TPU v7x, 256 devices: a whole 4x4x8 slice. The times are simulated.
256 devices in a mesh: layer: 8 (over x, y_hi), feat: 32 (over y_lo, z, core).
Axes of the slice: x: 4, y: 4 (y_hi: 2, y_lo: 2; y = y_hi * 2 + y_lo), z: 8, core: 2. Of those that a mesh axis runs over, the one named last changes fastest.
Arguments:
- inputs: bfloat16 [8, 512, 2048], P('layer', 'feat'), may hold values from -6 to 6
- targets: bfloat16 [8, 512, 2048], P('layer', 'feat'), may hold values from -6 to 6
- enc_weight: bfloat16 [8, 2048, 16384], P('layer', None, 'feat'), may hold values from -0.125 to 0.125
- enc_bias: float32 [8, 16384], P('layer', 'feat'), may hold values from -1 to 0.5
- dec_weight: bfloat16 [8, 2, 16384, 2048], P('layer', None, 'feat'), may hold values from -0.046875 to 0.046875
- dec_bias: float32 [8, 2048], P('layer'), may hold values from -3 to 3
Outputs:
- mean_loss: float32 [], replicated
- enc_grad: bfloat16 [8, 2048, 16384], P('layer', None, 'feat')
- enc_bias_grad: float32 [8, 16384], P('layer', 'feat')
- dec_grad: bfloat16 [8, 2, 16384, 2048], P('layer', None, 'feat')
- dec_bias_grad: float32 [8, 2048], P('layer')
All inputs are finite; a program needn't handle non-finite values.
Results may differ from a plain program's by a relative error of at most 0.006.
Values may be sent and summed in bfloat16 or wider, within the bound.
A program may use at most 128 MiB of HBM per device.

v0:
```python
import functools

import jax
import jax.numpy as jnp
from jax import lax
from jax.sharding import Mesh
from jax.sharding import PartitionSpec as P

FEAT = ("feat_0", "feat_1", "feat_2")
LAYER = ("layer_0", "layer_1")
LAYER_FEAT = ("layer_0", "layer_1", "feat_0", "feat_1", "feat_2")


def copy_for_each(value, axis):
    size = lax.axis_size(axis)
    return lax.all_to_all(
        jnp.broadcast_to(value[None], (size, *value.shape)), axis, 0, 0, tiled=True
    )


def joined_along(tiles, dim):
    lengths = list(tiles.shape[1:])
    lengths[dim] *= tiles.shape[0]
    return jnp.moveaxis(tiles, 0, dim).reshape(lengths)


def collect(value, axis, dim):
    tiles = copy_for_each(value, axis)
    return joined_along(tiles, dim)


def cut_along(value, dim, size):
    lengths = value.shape
    tiles = value.reshape(*lengths[:dim], size, lengths[dim] // size, *lengths[dim + 1 :])
    return jnp.moveaxis(tiles, dim, 0)


def scatter_pairs(value, chips, core, dim):
    sizes = (lax.axis_size(chips), lax.axis_size(core))
    tiles = cut_along(value, dim, sizes[0] * sizes[1])
    inside = tiles.shape[1:]
    tiles = tiles.reshape(*sizes, *inside).swapaxes(0, 1).reshape(-1, *inside)
    tiles = lax.psum_scatter(tiles, core, scatter_dimension=0, tiled=True)
    return lax.psum_scatter(tiles, chips, scatter_dimension=0, tiled=True)[0]


def passed_along(block, axis, distance):
    devices = range(lax.axis_size(axis))
    route = [(i - distance, i) for i in devices if i - distance in devices]
    return lax.ppermute(block, axis, route)


def one_axis_at_a_time(value, axes):
    return functools.reduce(lax.psum, axes, value)


def shards(inputs, targets, enc_weight, enc_bias, dec_weight, dec_bias):
    shard_rows = inputs.shape[1]
    reach = dec_weight.shape[1]
    width = dec_weight.shape[3]
    tokens_all = collect(inputs[0], FEAT, 0)
    pre = jnp.dot(tokens_all, enc_weight[0], preferred_element_type=jnp.float32) + enc_bias[0]
    acts = (jnp.maximum(pre, 0.0) ** 2).astype(jnp.bfloat16)
    out = jnp.einsum("tf,rfd->trd", acts, dec_weight[0], preferred_element_type=jnp.float32)
    summed = scatter_pairs(
        out.reshape(
            shard_rows * lax.axis_size(("feat_0", "feat_1")) * lax.axis_size("feat_2"),
            reach * width,
        ),
        ("feat_0", "feat_1"),
        "feat_2",
        0,
    )
    recon = summed[:, :width] + dec_bias[0]
    offset = 1
    recon = recon + passed_along(summed[:, offset * width : (offset + 1) * width], LAYER, offset)
    grad = (recon - targets[0].astype(jnp.float32)).astype(jnp.bfloat16)
    local_squares = jnp.sum(grad.astype(jnp.float32) ** 2)
    total = one_axis_at_a_time(local_squares, LAYER_FEAT)
    mean_loss = total / (lax.axis_size(LAYER) * lax.axis_size(FEAT) * shard_rows * width)
    pieces = [grad]
    offset = 1
    pieces.append(passed_along(grad, LAYER, -offset))
    stacked = jnp.stack(pieces, axis=1)
    gathered = lax.all_gather(stacked, FEAT, axis=0, tiled=True)
    fulls = [gathered[:, offset] for offset in range(reach)]
    dec_parts = []
    back = jnp.zeros(pre.shape, jnp.float32)
    for offset in range(reach):
        dec_parts.append(
            jnp.einsum("tf,td->fd", acts, fulls[offset], preferred_element_type=jnp.float32).astype(
                jnp.bfloat16
            )
        )
        back = back + jnp.einsum(
            "td,fd->tf", fulls[offset], dec_weight[0, offset], preferred_element_type=jnp.float32
        )
    dec_grad = jnp.stack(dec_parts, axis=0)
    dpre = (back * 2.0 * jnp.maximum(pre, 0.0)).astype(jnp.bfloat16)
    enc_grad = jnp.einsum("td,tf->df", tokens_all, dpre, preferred_element_type=jnp.float32).astype(
        jnp.bfloat16
    )
    enc_bias_grad = jnp.sum(dpre.astype(jnp.float32), axis=0)
    dec_bias_grad = jnp.sum(fulls[0].astype(jnp.float32), axis=0)
    return (mean_loss, enc_grad[None], enc_bias_grad[None], dec_grad[None], dec_bias_grad[None])


def solution(mesh):
    finer = Mesh(
        mesh.devices.reshape(4, 2, 2, 8, 2), ("layer_0", "layer_1", "feat_0", "feat_1", "feat_2")
    )
    placed = (
        P(LAYER, FEAT, None),
        P(LAYER, FEAT, None),
        P(LAYER, None, FEAT),
        P(LAYER, FEAT),
        P(LAYER, None, FEAT, None),
        P(LAYER, None),
    )
    return jax.shard_map(
        shards,
        mesh=finer,
        in_specs=placed,
        out_specs=(
            P(),
            P(LAYER, None, FEAT),
            P(LAYER, FEAT),
            P(LAYER, None, FEAT, None),
            P(LAYER, None),
        ),
        check_vma=False,
    )
```

profile of v0, /device:TPU:1, one launch (start us, length us, event | category | flops | bytes accessed | tf_op | source)
XLA Modules:
  0.0 300.6 jit_solution(5352324902528373081)
XLA Ops:
  7.2 2.6 broadcast_in_dim.20
  9.7 11.2 %all-to-all-start = ((bf16[32,16,2048]{2,1,0:T(8,128)(2,1)}), bf16[32,16,2048]{2,1,0:T(8,128)(2,1)}, u32[]{:S(2)}, u32[]{:S(2)}) async-start(bf16[32,16,2048]{2,1,0:T(8,128)(2,1)} %broadcast_in_dim.20), calls=%async_computation | async-start | bytes 4194304 | tf_op jit(solution)/shard_map/all_to_all | solution.py:16
  21.0 6.2 %copy.12 = bf16[1,2,512,2048]{2,3,1,0:T(8,128)(2,1)} copy(bf16[1,2,512,2048]{3,2,1,0:T(8,128)(2,1)} %param.10) | data formatting | bytes 8388608 | tf_op args[4]
  27.2 43.0 %all-to-all-done = bf16[32,16,2048]{2,1,0:T(8,128)(2,1)} async-done(((bf16[32,16,2048]{2,1,0:T(8,128)(2,1)}), bf16[32,16,2048]{2,1,0:T(8,128)(2,1)}, u32[]{:S(2)}, u32[]{:S(2)}) %all-to-all-start) | async-done | bytes 2097184 | tf_op jit(solution)/shard_map/all_to_all | solution.py:16
  70.2 4.0 %multiply_convert_fusion = (bf16[512,512]{1,0:T(8,128)(2,1)S(1)}, f32[512,512]{1,0:T(8,128)}) fusion(f32[512]{0:T(512)S(1)} %bitcast.97, bf16[512,2048]{1,0:T(8,128)(2,1)} %bitcast.1, bf16[1,2048,512]{2,1,0:T(8,128)(2,1)S(1)} %copy-done), kind=kOutput, calls=%fused_computation.26 | convolution fusion | flops 1074790400 | bytes 5769216 | tf_op jit(solution)/shard_map/dot_general | solution.py:62
  74.2 2.4 convolution_bitcast_fusion
  76.6 3.8 %copy.13 = f32[2,16,16,4096]{3,2,1,0:T(8,128)} copy(f32[2,16,16,4096]{3,2,0,1:T(8,128)S(1)} %convolution_bitcast_fusion) | data formatting | bytes 16777216 | tf_op jit(solution)/shard_map/transpose | solution.py:42
  80.5 21.5 %reduce-scatter.3.cloned.1.call-done = f32[16,16,4096]{2,1,0:T(8,128)} async-done(((f32[32,16,4096]{2,1,0:T(8,128)}), f32[16,16,4096]{2,1,0:T(8,128)}) %reduce-scatter.3.cloned.1.call-update) | async-done | bytes 4194320 | tf_op jit(solution)/shard_map/reduce_scatter | solution.py:43
  102.1 74.0 %reduce-scatter.5.cloned.1.call-done = f32[1,16,4096]{2,1,0:T(8,128)} async-done(((f32[16,16,4096]{2,1,0:T(8,128)}), f32[1,16,4096]{2,1,0:T(8,128)}) %reduce-scatter.5.cloned.1.call-update) | async-done | bytes 262160 | tf_op jit(solution)/shard_map/reduce_scatter | solution.py:44
  176.9 4.4 %collective-permute-start = (f32[16,2048]{1,0:T(8,128)S(1)}, f32[16,2048]{1,0:T(8,128)S(1)}, u32[]{:S(2)}, u32[]{:S(2)}) collective-permute-start(f32[16,2048]{1,0:T(8,128)S(1)} %slice.25), channel_id=1, source_target_pairs={{0,32},{32,64},{64,96},{96,128},{128,160},{160,192},{192,224},{1,3... | collective-permute-start | bytes 393224 | tf_op jit(solution)/shard_map/ppermute | solution.py:50
  181.3 3.3 %collective-permute-done = f32[16,2048]{1,0:T(8,128)S(1)} collective-permute-done((f32[16,2048]{1,0:T(8,128)S(1)}, f32[16,2048]{1,0:T(8,128)S(1)}, u32[]{:S(2)}, u32[]{:S(2)}) %collective-permute-start) | collective-permute-done | bytes 131104 | tf_op jit(solution)/shard_map/ppermute | solution.py:50
  187.5 6.1 %collective-permute-done.1 = bf16[16,2048]{1,0:T(8,128)(2,1)S(1)} collective-permute-done((bf16[16,2048]{1,0:T(8,128)(2,1)S(1)}, bf16[16,2048]{1,0:T(8,128)(2,1)S(1)}, u32[]{:S(2)}, u32[]{:S(2)}) %collective-permute-start.1) | collective-permute-done | bytes 65568 | tf_op jit(solution)/shard_map/ppermute | solution.py:50
  194.2 9.7 %psum.35 = f32[]{:T(128)} all-reduce(f32[]{:T(128)} %get-tuple-element.15), channel_id=1, replica_groups=mesh['layer_0'=4,'layer_1'=2,'feat_0'=2,'feat_1'=8,'feat_2'=2] {'layer_0'}, use_global_device_ids=true, to_apply=%region_3.0 | all-reduce | flops 1 | bytes 8 | tf_op jit(solution)/shard_map/psum | solution.py:54
  203.9 5.9 %psum.36 = f32[]{:T(128)} all-reduce(f32[]{:T(128)} %psum.35), channel_id=1, replica_groups=mesh['layer_0'=4,'layer_1'=2,'feat_0'=2,'feat_1'=8,'feat_2'=2] {'layer_1'}, use_global_device_ids=true, to_apply=%region_4.0 | all-reduce | flops 1 | bytes 8 | tf_op jit(solution)/shard_map/psum | solution.py:54
  209.8 4.4 %psum.37 = f32[]{:T(128)} all-reduce(f32[]{:T(128)} %psum.36), channel_id=1, replica_groups=mesh['layer_0'=4,'layer_1'=2,'feat_0'=2,'feat_1'=8,'feat_2'=2] {'feat_0'}, use_global_device_ids=true, to_apply=%region_5.0 | all-reduce | flops 1 | bytes 8 | tf_op jit(solution)/shard_map/psum | solution.py:54
  214.2 11.8 %psum.38 = f32[]{:T(128)} all-reduce(f32[]{:T(128)} %psum.37), channel_id=1, replica_groups=mesh['layer_0'=4,'layer_1'=2,'feat_0'=2,'feat_1'=8,'feat_2'=2] {'feat_1'}, use_global_device_ids=true, to_apply=%region_6.0 | all-reduce | flops 1 | bytes 8 | tf_op jit(solution)/shard_map/psum | solution.py:54
  226.0 22.7 %psum.39 = f32[]{:T(128)} all-reduce(f32[]{:T(128)} %psum.38), channel_id=1, replica_groups=mesh['layer_0'=4,'layer_1'=2,'feat_0'=2,'feat_1'=8,'feat_2'=2] {'feat_2'}, use_global_device_ids=true, to_apply=%region_7.0 | all-reduce | flops 1 | bytes 8 | tf_op jit(solution)/shard_map/psum | solution.py:54
  249.4 20.9 %all-gather.2.cloned.1.call-done = bf16[512,2,2048]{2,0,1:T(8,128)(2,1)} async-done(((bf16[16,2,2048]{2,0,1:T(8,128)(2,1)}), bf16[512,2,2048]{2,0,1:T(8,128)(2,1)}) %all-gather.2.cloned.1.call-update) | async-done | bytes 4194320 | tf_op jit(solution)/shard_map/all_gather | solution.py:85
  270.3 3.7 %fusion.3 = f32[512,512]{1,0:T(8,128)S(1)} fusion(bf16[1,2,512,2048]{3,2,1,0:T(8,128)(2,1)} %param.10, bf16[512,2,2048]{2,0,1:T(8,128)(2,1)} %all-gather.2.cloned.1.call-done), kind=kOutput, calls=%fused_computation.11 | convolution fusion | flops 1073741824 | bytes 5242880 | tf_op jit(solution)/shard_map/td,fd->tf/dot_general | solution.py:95
  275.2 1.9 convert_reduce_fusion.1
  277.1 4.2 %fusion = bf16[1,2048,512]{1,2,0:T(8,128)(2,1)} fusion(bf16[512,512]{1,0:T(8,128)(2,1)S(1)} %get-tuple-element.20, bf16[512,2048]{1,0:T(8,128)(2,1)} %bitcast.1), kind=kOutput, calls=%fused_computation.6 | convolution fusion | flops 1074790400 | bytes 4718592 | tf_op jit(solution)/shard_map/td,tf->df/dot_general | solution.py:100
  281.3 3.9 %copy.14 = bf16[1,2048,512]{2,1,0:T(8,128)(2,1)} copy(bf16[1,2048,512]{1,2,0:T(8,128)(2,1)} %fusion) | data formatting | bytes 4194304
  285.2 3.0 %fusion.1 = bf16[1,512,2048]{2,1,0:T(8,128)(2,1)S(1)} fusion(bf16[512,512]{1,0:T(8,128)(2,1)S(1)} %get-tuple-element.17, bf16[512,2,2048]{2,0,1:T(8,128)(2,1)} %all-gather.2.cloned.1.call-done), kind=kOutput, calls=%fused_computation.7 | convolution fusion | flops 1074790400 | bytes 4718592 | tf_op jit(solution)/shard_map/tf,td->fd/dot_general | solution.py:91
  289.5 2.4 maximum_bitcast_fusion
  (30 shorter events, 8.1 us)
Async XLA Ops:
  7.2 63.1 %copy-start = (bf16[1,2048,512]{2,1,0:T(8,128)(2,1)S(1)}, bf16[1,2048,512]{2,1,0:T(8,128)(2,1)}, u32[]{:S(2)}) copy-start(bf16[1,2048,512]{2,1,0:T(8,128)(2,1)} %param.8) | copy-start | bytes 6291460
  9.7 60.5 %all-to-all-start = ((bf16[32,16,2048]{2,1,0:T(8,128)(2,1)}), bf16[32,16,2048]{2,1,0:T(8,128)(2,1)}, u32[]{:S(2)}, u32[]{:S(2)}) async-start(bf16[32,16,2048]{2,1,0:T(8,128)(2,1)} %broadcast_in_dim.20), calls=%async_computation | async-start | bytes 4194304 | tf_op jit(solution)/shard_map/all_to_all | solution.py:16
  20.9 49.3 %copy-start.7 = (f32[1,512]{1,0:T(1,128)S(1)}, f32[1,512]{1,0:T(1,128)}, u32[]{:S(2)}) copy-start(f32[1,512]{1,0:T(1,128)} %param.9) | copy-start | bytes 6148
  20.9 81.0 %reduce-scatter.3.cloned.1.call-start = ((), (), s32[]{:S(2)}) async-start(), calls=%async_computation.3 | async-start | bytes 12582912 | tf_op jit(solution)/shard_map/reduce_scatter | solution.py:43
  70.2 4.0 %copy-start.2 = (bf16[1,2,512,2048]{2,3,1,0:T(8,128)(2,1)S(1)}, bf16[1,2,512,2048]{2,3,1,0:T(8,128)(2,1)}, u32[]{:S(2)}) copy-start(bf16[1,2,512,2048]{2,3,1,0:T(8,128)(2,1)} %copy.12) | copy-start | bytes 12582916
  80.4 95.6 %reduce-scatter.5.cloned.1.call-start = ((), (), s32[]{:S(2)}) async-start(), calls=%async_computation.4 | async-start | bytes 4456448 | tf_op jit(solution)/shard_map/reduce_scatter | solution.py:44
  102.0 82.6 %copy-start.5 = (bf16[1,16,2048]{2,1,0:T(8,128)(2,1)S(1)}, bf16[1,16,2048]{2,1,0:T(8,128)(2,1)}, u32[]{:S(2)}) copy-start(bf16[1,16,2048]{2,1,0:T(8,128)(2,1)} %param.7) | copy-start | bytes 196612
  102.0 82.6 %copy-start.6 = (f32[1,2048]{1,0:T(1,128)S(1)}, f32[1,2048]{1,0:T(1,128)}, u32[]{:S(2)}) copy-start(f32[1,2048]{1,0:T(1,128)} %param.11) | copy-start | bytes 24580
  102.0 168.2 %all-gather.2.cloned.1.call-start = ((), (), s32[]{:S(2)}) async-start(), calls=%async_computation.5 | async-start | bytes 4325376 | tf_op jit(solution)/shard_map/all_gather | solution.py:85
  176.9 7.7 %collective-permute-start = (f32[16,2048]{1,0:T(8,128)S(1)}, f32[16,2048]{1,0:T(8,128)S(1)}, u32[]{:S(2)}, u32[]{:S(2)}) collective-permute-start(f32[16,2048]{1,0:T(8,128)S(1)} %slice.25), channel_id=1, source_target_pairs={{0,32},{32,64},{64,96},{96,128},{128,160},{160,192},{192,224},{1,3... | collective-permute-start | bytes 393224 | tf_op jit(solution)/shard_map/ppermute | solution.py:50
  186.2 7.4 %collective-permute-start.1 = (bf16[16,2048]{1,0:T(8,128)(2,1)S(1)}, bf16[16,2048]{1,0:T(8,128)(2,1)S(1)}, u32[]{:S(2)}, u32[]{:S(2)}) collective-permute-start(bf16[16,2048]{1,0:T(8,128)(2,1)S(1)} %get-tuple-element.16), channel_id=1, source_target_pairs={{32,0},{64,32},{96,64},{128,96},{160,128},{192,160},{224,192},{33,... | collective-permute-start | bytes 196616 | tf_op jit(solution)/shard_map/ppermute | solution.py:50
  270.3 3.7 %copy-start.1 = (bf16[1,2,512,2048]{3,2,1,0:T(8,128)(2,1)S(1)}, bf16[1,2,512,2048]{3,2,1,0:T(8,128)(2,1)}, u32[]{:S(2)}) copy-start(bf16[1,2,512,2048]{3,2,1,0:T(8,128)(2,1)} %param.10) | copy-start | bytes 12582916
  270.3 4.7 %copy-start.3 = (bf16[512,2,2048]{2,0,1:T(8,128)(2,1)S(1)}, bf16[512,2,2048]{2,0,1:T(8,128)(2,1)}, u32[]{:S(2)}) copy-start(bf16[512,2,2048]{2,0,1:T(8,128)(2,1)} %all-gather.2.cloned.1.call-done) | copy-start | bytes 12582916
  270.3 4.9 %copy-start.8 = (f32[512,512]{1,0:T(8,128)S(1)}, f32[512,512]{1,0:T(8,128)}, u32[]{:S(2)}) copy-start(f32[512,512]{1,0:T(8,128)} %get-tuple-element.18) | copy-start | bytes 3145732
  285.2 3.0 %copy-start.4 = (bf16[512,2,2048]{2,0,1:T(8,128)(2,1)S(1)}, bf16[512,2,2048]{2,0,1:T(8,128)(2,1)}, u32[]{:S(2)}) copy-start(bf16[512,2,2048]{2,0,1:T(8,128)(2,1)} %all-gather.2.cloned.1.call-done) | copy-start | bytes 12582916
Sparse Core Ops, SparseCore 0:
  80.5 21.3 reduce-scatter.2
  104.5 71.4 reduce-scatter.4
  194.4 75.8 all-gather.1
where the time goes:
time: 301 us
  waiting for transfers between devices  169 us (56%)
  blocking collectives  54.5 us (18%)
  matrix products  20.4 us (7%)
  local copies, waits for them, and re-layouts  18.7 us (6%)
  starting transfers between devices  17 us (6%)
  between operations  15.6 us (5%)
  other arithmetic  5.57 us (2%)
    reduce_scatter x1, waiting for transfers between devices, scatter_pairs(): return lax.psum_scatter(tiles, chips, scatter_dimension=0, tiled=True)[0]  74 us
    psum x5, blocking collectives, one_axis_at_a_time(): return functools.reduce(lax.psum, axes, value)  54.5 us
    all_to_all x1, waiting for transfers between devices, copy_for_each(): lax.all_to_all(jnp.broadcast_to(value[None], (size, *value.shape)), axis,...  43 us
    reduce_scatter x1, waiting for transfers between devices, scatter_pairs(): tiles = lax.psum_scatter(tiles, core, scatter_dimension=0, tiled=True)  21.5 us
    all_gather x1, waiting for transfers between devices, shards(): gathered = lax.all_gather(stacked, FEAT, axis=0, tiled=True)  20.9 us
    unnamed x20, local copies, waits for them, and re-layouts  11.4 us
    all_to_all x1, starting transfers between devices, copy_for_each(): lax.all_to_all(jnp.broadcast_to(value[None], (size, *value.shape)), axis,...  11.2 us
    ppermute x2, waiting for transfers between devices, passed_along(): return lax.ppermute(block, axis, route)  9.36 us
  transfers between devices with their start and end apart: 6, of which 6 were waited for; matrix products, arithmetic and copies ran while one was open for 2% of the time, Pallas kernels for 0%

commit v1 on v0

v1 whole, which is shorter than its diff:
```python
import jax
import jax.numpy as jnp
from jax import lax
from jax.experimental import pallas as pl
from jax.experimental.pallas import tpu as pltpu
from jax.sharding import Mesh
from jax.sharding import PartitionSpec as P

MESH = pl.DeviceIdType.MESH
BF16, F32 = jnp.bfloat16, jnp.float32
LAYER = ("x", "yh")
FEAT = ("yl", "z", "c")
NX, NZ = 4, 8

BLOCKS = (
    ((0, 0), (1, 0), (0, 1), (0, -1)),
    ((0, 2), (0, -2), (1, 1), (1, -1)),
    ((0, 3), (0, -3), (1, 2), (1, -2)),
    ((0, 4), (1, 3), (1, -3), (1, 4)),
)
PLACE = {slot: (b, k) for b, block in enumerate(BLOCKS) for k, slot in enumerate(block)}
OWN = (0, 0)
WAVES = (
    (OWN,),
    ((0, 1), (0, -1), (1, 0)),
    ((0, 2), (0, -2), (1, 1), (1, -1)),
    ((0, 3), (0, -3), (1, 2), (1, -2)),
    ((0, 4), (1, 3), (1, -3)),
    ((1, 4),),
)


def parent_of(slot, half):
    dy, dz = slot
    if dy == 1 and dz in (0, 3, -3, 4):
        return (0, dz), "y"
    if dz == 4:
        return ((0, 3), "+") if half == 0 else ((0, -3), "-")
    return ((dy, dz - 1), "+") if dz > 0 else ((dy, dz + 1), "-")


SLOTS = tuple(slot for block in BLOCKS for slot in block)
CHILDREN = {
    (half, slot): tuple(c for c in SLOTS if c != OWN and parent_of(c, half)[0] == slot)
    for half in (0, 1)
    for slot in SLOTS
}


def mirrored(slot, half):
    dy, dz = slot
    return (dy, dz) if half == 0 or dz == 4 else (dy, -dz)


REDUCE = (
    ((1, 4), (1, 3), (1, -3), (1, 2), (1, -2)),
    ((0, 4), (0, -3), (1, 1), (1, -1)),
    ((0, 3), (0, -2), (1, 0)),
    ((0, 2), (0, -1)),
    ((0, 1),),
)


def main_kernel(
    x_hbm, t_hbm, ew_hbm, eb_hbm, dw_hbm, db_hbm,
    tok_o, acts_o, grads_o, dpre_o, sums_o, loss_o,
    tok, ew, dw, eb, db, tg, pre, acts, part, sib_out, sib_in, arr, snd, shift_out, shift_in,
    gshift_in, gr, back, dpre, sums, squares, loss_all, loss_sum,
    load_sem, store_sem, tok_s, tok_r, tsib_s, tsib_r, psib_s, psib_r, red_s, red_r,
    sh_s, sh_r, gr_s, gr_r, gsib_s, gsib_r, loss_s, loss_r,
):
    x, yh = lax.axis_index("x"), lax.axis_index("yh")
    yl, z, c = lax.axis_index("yl"), lax.axis_index("z"), lax.axis_index("c")
    layer = x * 2 + yh
    width = dw.shape[2]
    half_width = width // 2

    to = {
        "+": {"z": lax.rem(z + 1, NZ)},
        "-": {"z": lax.rem(z + NZ - 1, NZ)},
        "y": {"yl": 1 - yl},
    }
    back_to = {"+": to["-"], "-": to["+"], "y": to["y"]}
    sibling = {"c": 1 - c}
    following = {"x": lax.rem(x + yh, NX), "yh": 1 - yh}
    previous = {"x": lax.rem(x + yh + NX - 1, NX), "yh": 1 - yh}
    peers = [
        {"x": lax.rem(x + k // 2, NX), "yh": lax.rem(yh + k % 2, 2)} for k in range(1, 2 * NX)
    ]

    def load(k, src, dst):
        copy = pltpu.make_async_copy(src, dst, load_sem.at[k])
        copy.start()
        return copy

    own_loads = [
        load(h, x_hbm.at[0, :, pl.ds(h * half_width, half_width)], tok.at[h, 0, 0, 0])
        for h in (0, 1)
    ]
    ew_load = load(2, ew_hbm.at[0], ew)
    eb_load = load(3, eb_hbm, eb)
    dw_loads = [load(4 + r, dw_hbm.at[0, r], dw.at[r]) for r in (1, 0)]
    tg_load = load(6, t_hbm.at[0], tg)
    db_load = load(7, db_hbm, db)

    barrier = pltpu.get_barrier_semaphore()
    greeted = [to["+"], to["-"], to["y"], sibling, following, previous, *peers]
    for device in greeted:
        pl.semaphore_signal(barrier, inc=1, device_id=device, device_id_type=MESH)
    pl.semaphore_wait(barrier, len(greeted))

    def remote(src, dst, send_sem, recv_sem, device):
        return pltpu.make_async_remote_copy(
            src_ref=src, dst_ref=dst, send_sem=send_sem, recv_sem=recv_sem,
            device_id=device, device_id_type=MESH,
        )

    sent = []

    def gather(buf, ici_s, ici_r, sib_s, sib_r):
        ici, sib = {}, {}
        for h in (0, 1):
            for s in SLOTS:
                b, k = PLACE[s]
                sib[h, s] = remote(
                    buf.at[h, b, 0, k], buf.at[h, b, 1, k],
                    sib_s.at[h, b, k], sib_r.at[h, b, k], sibling,
                )
                if s == OWN:
                    continue
                parent, way = parent_of(s, h)
                pb, pk = PLACE[parent]
                ici[h, s] = remote(
                    buf.at[h, pb, 0, pk], buf.at[h, b, 0, k],
                    ici_s.at[h, b, k], ici_r.at[h, b, k], to[way],
                )

        def stage(n, h):
            for s in WAVES[n]:
                if s != OWN:
                    ici[h, s].wait_recv()
                for child in CHILDREN[h, s]:
                    ici[h, child].start()
                    sent.append(ici[h, child])
                sib[h, s].start()
                sent.append(sib[h, s])

        def settle(b, h):
            for s in BLOCKS[b]:
                sib[h, s].wait_recv()

        return stage, settle

    stage, settle = gather(tok, tok_s, tok_r, tsib_s, tsib_r)

    def encode(b):
        rows = pl.ds(b * 128, 128)
        for h in (0, 1):
            settle(b, h)
        value = eb[...] + jnp.zeros((128, 1), F32)
        for h in (0, 1):
            value += jnp.dot(
                tok[h, b].reshape(128, half_width),
                ew[h * half_width : (h + 1) * half_width],
                preferred_element_type=F32,
            )
        value = jnp.maximum(value, 0.0)
        pre[rows] = value
        acts[rows] = (value * value).astype(BF16)

    for h in (0, 1):
        own_loads[h].wait()
        stage(0, h)
    for n in (1, 2):
        for h in (0, 1):
            stage(n, h)
    ew_load.wait()
    eb_load.wait()
    encode(0)
    for n in (3, 4, 5):
        for h in (0, 1):
            stage(n, h)
        encode(n - 2)
    stores = []

    def store(src, dst):
        copy = pltpu.make_async_copy(src, dst, store_sem.at[len(stores)])
        copy.start()
        stores.append(copy)

    store(tok, tok_o)
    store(acts, acts_o)

    psib = {
        (h, b): remote(
            sib_out.at[h, b], sib_in.at[h, b], psib_s.at[h, b], psib_r.at[h, b], sibling
        )
        for h in (0, 1)
        for b in range(4)
    }
    tile = 512

    def decode(b):
        lhs = acts[pl.ds(b * 128, 128)]
        for h in (0, 1):

            @pl.loop(0, width // tile)
            def _(j):
                columns = pl.ds(pl.multiple_of(j * tile, tile), tile)
                value = jnp.dot(lhs, dw[1 - h, :, columns], preferred_element_type=F32)
                part[h, b, :, :, columns] = value[:64].reshape(4, 16, tile)
                sib_out[h, b, :, :, columns] = value[64:].astype(BF16).reshape(4, 16, tile)

            psib[h, b].start()
            sent.append(psib[h, b])

    red = {}
    for h in (0, 1):
        for s in SLOTS[1:]:
            b, k = PLACE[s]
            red[h, s] = remote(
                snd.at[h, b, k], arr.at[h, b, k], red_s.at[h, b, k], red_r.at[h, b, k],
                back_to[parent_of(s, h)[1]],
            )

    def total(h, s):
        b, k = PLACE[s]
        value = part[h, b, k] + sib_in[h, b, k].astype(F32)
        for child in CHILDREN[h, s]:
            red[h, child].wait_recv()
            cb, ck = PLACE[child]
            value += arr[h, cb, ck].astype(F32)
        return value

    def pass_on(h, s):
        b, k = PLACE[s]
        snd[h, b, k] = total(h, s).astype(BF16)
        red[h, s].start()
        sent.append(red[h, s])

    for load_ in dw_loads:
        load_.wait()
    decode(3)
    decode(2)
    for h in (0, 1):
        psib[h, 3].wait_recv()
        psib[h, 2].wait_recv()
        for s in REDUCE[0]:
            pass_on(h, mirrored(s, h))
    decode(1)
    for h in (0, 1):
        psib[h, 1].wait_recv()
        for s in REDUCE[1]:
            pass_on(h, mirrored(s, h))
    decode(0)
    for h in (0, 1):
        psib[h, 0].wait_recv()
        for s in REDUCE[2]:
            pass_on(h, mirrored(s, h))
    for n in (3, 4):
        for h in (0, 1):
            for s in REDUCE[n]:
                pass_on(h, mirrored(s, h))
    shift_out[...] = total(0, OWN).astype(BF16)
    shift = remote(shift_out, shift_in, sh_s.at[0], sh_r.at[0], following)
    shift.start()
    tg_load.wait()
    db_load.wait()
    recon = total(1, OWN) + db[...] - tg[...].astype(F32)
    shift.wait_recv()
    recon += jnp.where(layer == 0, 0.0, shift_in[...].astype(F32))
    gr[0, 0, 0, 0] = recon.astype(BF16)
    gshift = remote(gr.at[0, 0, 0, 0], gshift_in, sh_s.at[1], sh_r.at[1], previous)
    gshift.start()
    sent += [shift, gshift]

    stage, settle = gather(gr, gr_s, gr_r, gsib_s, gsib_r)

    def through(b, h):
        rows = pl.ds(b * 128, 128)
        settle(b, h)
        value = lax.dot_general(
            gr[h, b].reshape(128, width), dw[h], (((1,), (1,)), ((), ())),
            preferred_element_type=F32,
        )
        if h == 0:
            back[rows] = value
        else:
            value += back[rows]
            dpre[rows] = (value * 2.0 * pre[rows]).astype(BF16)

    def add_up():
        @pl.loop(0, width // tile)
        def _(j):
            columns = pl.ds(pl.multiple_of(j * tile, tile), tile)
            total_sum = jnp.zeros((8, tile), F32)
            total_sq = jnp.zeros((8, tile), F32)
            for b in range(4):
                for p in range(2):
                    value = gr[0, b, p, :, :, columns].astype(F32).reshape(8, 8, tile)
                    total_sum += jnp.sum(value, axis=0)
                    total_sq += jnp.sum(value * value, axis=0)
            sums[:, columns] = total_sum
            squares[:, columns] = total_sq

        value = jnp.zeros((8, 128), F32)
        for j in range(width // 128):
            value += squares[:, j * 128 : (j + 1) * 128]
        loss_all[0] = value
        store(sums, sums_o)

    stage(0, 0)
    stage(1, 0)
    gshift.wait_recv()
    gr[1, 0, 0, 0] = jnp.where(layer == 2 * NX - 1, 0.0, gshift_in[...].astype(F32)).astype(BF16)
    stage(0, 1)
    stage(2, 0)
    stage(1, 1)
    through(0, 0)
    stage(3, 0)
    stage(2, 1)
    through(1, 0)
    stage(4, 0)
    stage(3, 1)
    through(2, 0)
    stage(5, 0)
    through(0, 1)
    stage(4, 1)
    through(3, 0)
    store(gr.at[0], grads_o.at[0])
    stage(5, 1)
    add_up()
    tells = []
    for k, device in enumerate(peers):
        tells.append(
            remote(loss_all.at[0], loss_all.at[k + 1], loss_s.at[k], loss_r.at[k], device)
        )
        tells[-1].start()
    for b in (1, 2, 3):
        through(b, 1)
    store(gr.at[1], grads_o.at[1])
    store(dpre, dpre_o)
    for tell in tells:
        tell.wait_recv()
    sent += tells
    value = loss_all[0]
    for k in range(1, 2 * NX):
        value += loss_all[k]
    loss_sum[...] = value
    store(loss_sum, loss_o)
    for copy in sent:
        copy.wait_send()
    for copy in stores:
        copy.wait()


def grad_kernel(scale, tok, acts, dpre, grads, sums, loss, eg, ebg, dg, dbg, mean):
    contract = (((0,), (0,)), ((), ()))
    eg[0] = lax.dot_general(tok[0], dpre[...], contract, preferred_element_type=F32).astype(BF16)
    dg[0, 0] = lax.dot_general(acts[...], grads[0], contract, preferred_element_type=F32).astype(
        BF16
    )

    @pl.when(pl.program_id(0) == 0)
    def _():
        ebg[...] = jnp.sum(dpre[...].astype(F32), axis=0, keepdims=True)
        dbg[...] = jnp.sum(sums[...], axis=0, keepdims=True)
        mean[0, 0] = jnp.sum(loss[...]) * scale


def shards(inputs, targets, enc_weight, enc_bias, dec_weight, dec_bias):
    rows, width = inputs.shape[1:]
    feats = enc_weight.shape[2]
    tokens = rows * 32
    half_width = width // 2
    anywhere = pl.BlockSpec(memory_space=pl.ANY)
    dma = pltpu.SemaphoreType.DMA
    tok, acts, grads, dpre, sums, loss = pl.pallas_call(
        main_kernel,
        out_shape=(
            jax.ShapeDtypeStruct((2, 4, 2, 4, rows, half_width), BF16),
            jax.ShapeDtypeStruct((tokens, feats), BF16),
            jax.ShapeDtypeStruct((2, 4, 2, 4, rows, width), BF16),
            jax.ShapeDtypeStruct((tokens, feats), BF16),
            jax.ShapeDtypeStruct((8, width), F32),
            jax.ShapeDtypeStruct((8, 128), F32),
        ),
        in_specs=[anywhere] * 6,
        out_specs=(anywhere,) * 6,
        scratch_shapes=[
            pltpu.VMEM((2, 4, 2, 4, rows, half_width), BF16),
            pltpu.VMEM((width, feats), BF16),
            pltpu.VMEM((2, feats, width), BF16),
            pltpu.VMEM((1, feats), F32),
            pltpu.VMEM((1, width), F32),
            pltpu.VMEM((rows, width), BF16),
            pltpu.VMEM((tokens, feats), F32),
            pltpu.VMEM((tokens, feats), BF16),
            pltpu.VMEM((2, 4, 4, rows, width), F32),
            pltpu.VMEM((2, 4, 4, rows, width), BF16),
            pltpu.VMEM((2, 4, 4, rows, width), BF16),
            pltpu.VMEM((2, 4, 4, rows, width), BF16),
            pltpu.VMEM((2, 4, 4, rows, width), BF16),
            pltpu.VMEM((rows, width), BF16),
            pltpu.VMEM((rows, width), BF16),
            pltpu.VMEM((rows, width), BF16),
            pltpu.VMEM((2, 4, 2, 4, rows, width), BF16),
            pltpu.VMEM((tokens, feats), F32),
            pltpu.VMEM((tokens, feats), BF16),
            pltpu.VMEM((8, width), F32),
            pltpu.VMEM((8, width), F32),
            pltpu.VMEM((2 * NX, 8, 128), F32),
            pltpu.VMEM((8, 128), F32),
            dma((8,)),
            dma((8,)),
            *[dma((2, 4, 4))] * 4,
            *[dma((2, 4))] * 2,
            *[dma((2, 4, 4))] * 2,
            *[dma((2,))] * 2,
            *[dma((2, 4, 4))] * 4,
            *[dma((2 * NX - 1,))] * 2,
        ],
        compiler_params=pltpu.CompilerParams(
            collective_id=0, has_side_effects=True, vmem_limit_bytes=60 * 2**20
        ),
        name="exchange",
    )(inputs, targets, enc_weight, enc_bias, dec_weight, dec_bias)
    tok = tok.reshape(2, tokens, half_width)
    grads = grads.reshape(2, tokens, width)
    whole = lambda *shape: pl.BlockSpec(shape, lambda i: (0,) * len(shape))
    eg, ebg, dg, dbg, mean = pl.pallas_call(
        lambda *refs: grad_kernel(1.0 / (2 * NX * tokens * width), *refs),
        grid=(8,),
        out_shape=(
            jax.ShapeDtypeStruct((1, width, feats), BF16),
            jax.ShapeDtypeStruct((1, feats), F32),
            jax.ShapeDtypeStruct((1, 2, feats, width), BF16),
            jax.ShapeDtypeStruct((1, width), F32),
            jax.ShapeDtypeStruct((1, 1), F32),
        ),
        in_specs=[
            pl.BlockSpec((1, tokens, width // 8), lambda i: (i // 4, 0, i % 4)),
            whole(tokens, feats),
            whole(tokens, feats),
            pl.BlockSpec((1, tokens, width // 4), lambda i: (i // 4, 0, i % 4)),
            whole(8, width),
            whole(8, 128),
        ],
        out_specs=(
            pl.BlockSpec((1, width // 8, feats), lambda i: (0, i, 0)),
            whole(1, feats),
            pl.BlockSpec((1, 1, feats, width // 4), lambda i: (0, i // 4, 0, i % 4)),
            whole(1, width),
            pl.BlockSpec(memory_space=pltpu.SMEM),
        ),
        name="weight_grads",
    )(tok, acts, dpre, grads, sums, loss)
    return mean[0, 0], eg, ebg, dg, dbg


def solution(mesh):
    finer = Mesh(mesh.devices.reshape(NX, 2, 2, NZ, 2), LAYER + FEAT)
    return jax.shard_map(
        shards,
        mesh=finer,
        in_specs=(
            P(LAYER, FEAT, None),
            P(LAYER, FEAT, None),
            P(LAYER, None, FEAT),
            P(LAYER, FEAT),
            P(LAYER, None, FEAT, None),
            P(LAYER, None),
        ),
        out_specs=(
            P(),
            P(LAYER, None, FEAT),
            P(LAYER, FEAT),
            P(LAYER, None, FEAT, None),
            P(LAYER, None),
        ),
        check_vma=False,
    )
```

time: 301 us -> 105 us (0.35)
  waiting for transfers between devices: 169 us -> 0 us
  Pallas kernels: 0 us -> 102 us
  blocking collectives: 54.5 us -> 0 us
  matrix products: 20.4 us -> 0 us
  local copies, waits for them, and re-layouts: 18.7 us -> 0 us
  starting transfers between devices: 17 us -> 0 us
  between operations: 15.6 us -> 0.64 us
  other arithmetic: 5.57 us -> 0 us
    pallas_call x0 -> x2, Pallas kernels: none -> 102 us  [the longest x1 92.2 us: shards(): pl.pallas_call(main_kernel, out_shape=(jax.ShapeDtypeStruct((2, 4, 2, 4,...]
    reduce_scatter x2 -> x0, waiting for transfers between devices: 95.5 us -> none  [the longest x1 74 us: scatter_pairs(): return lax.psum_scatter(tiles, chips, scatter_dimension=0, tiled=True)[0]]
    psum x5 -> x0, blocking collectives: 54.5 us -> none  [one_axis_at_a_time(): return functools.reduce(lax.psum, axes, value)]
    all_to_all x1 -> x0, waiting for transfers between devices: 43 us -> none  [copy_for_each(): lax.all_to_all(jnp.broadcast_to(value[None], (size, *value.shape)), axis,...]
    all_gather x1 -> x0, waiting for transfers between devices: 20.9 us -> none  [shards(): gathered = lax.all_gather(stacked, FEAT, axis=0, tiled=True)]
    dot_general x7 -> x0, matrix products: 20.4 us -> none  [the longest x2 5.55 us: shards(): jnp.einsum('td,fd->tf', fulls[offset], dec_weight[0, offset], preferred_e...]
    unnamed x20 -> x0, local copies, waits for them, and re-layouts: 11.4 us -> none
    all_to_all x1 -> x0, starting transfers between devices: 11.2 us -> none  [copy_for_each(): lax.all_to_all(jnp.broadcast_to(value[None], (size, *value.shape)), axis,...]
  transfers between devices with their start and end apart: 6 -> 0, of which waited for: 6 -> 0; matrix products, arithmetic and copies ran while one was open for 2% -> 0% of each run, Pallas kernels for 0% -> 0%
where the time goes in v1:
time: 105 us; the launch traced here: 103 us
  Pallas kernels  102 us (97%)
    pallas_call x1, Pallas kernels, shards(): pl.pallas_call(main_kernel, out_shape=(jax.ShapeDtypeStruct((2, 4, 2, 4,...  92.2 us
    pallas_call x1, Pallas kernels, shards(): pl.pallas_call(lambda *refs: grad_kernel(1.0 / (2 * NX * tokens * width),...  10.1 us

profile of v1, /device:TPU:1, one launch (start us, length us, event | category | flops | bytes accessed | tf_op | source)
XLA Modules:
  0.0 103.0 jit_solution(10193940241484423358)
XLA Ops:
  0.6 92.2 %exchange.1 = (bf16[2,4,2,4,16,1024]{5,4,3,2,1,0:T(8,128)(2,1)}, bf16[512,512]{1,0:T(8,128)(2,1)}, bf16[2,4,2,4,16,2048]{5,4,3,2,1,0:T(8,128)(2,1)}, bf16[512,51...) custom-call(bf16[1,16,2048]{2,1,0:T(8,128)(2,1)} %x_hbm.1, bf16[1,16,2048]{2,1,0:T(8,128)(2,1)} %t_hbm.1, ...), custom_call_target="tpu_custom_call" | custom-call | tf_op jit(solution)/shard_map/exchange/pallas_call | solution.py:378
  92.9 10.1 %weight_grads.1 = (bf16[1,2048,512]{2,1,0:T(8,128)(2,1)}, f32[1,512]{1,0:T(1,128)}, bf16[1,2,512,2048]{3,2,1,0:T(8,128)(2,1)}, f32[1,2048]{1,0:T(1,128)}, f32[1,1]{1,0:T(1,128)}) custom-call(bf16[2,512,1024]{2,1,0:T(8,128)(2,1)} %bitcast.4, bf16[512,512]{1,0:T(8,128)(2,1)} %get-tuple-element.17.refs_1_, bf16[512,512]{1,0:T(8,128)(2,1)} %get-tuple-element.18.refs_2_, ...), custom_call_target="tpu_custom_call" | custom-call | tf_op jit(solution)/shard_map/weight_grads/pallas_call | solution.py:431

commit v2 on v1

v2 whole, which is shorter than its diff:
```python
import jax
import jax.numpy as jnp
from jax import lax
from jax.experimental import pallas as pl
from jax.experimental.pallas import tpu as pltpu
from jax.sharding import Mesh
from jax.sharding import PartitionSpec as P

MESH = pl.DeviceIdType.MESH
BF16, F32 = jnp.bfloat16, jnp.float32
LAYER = ("x", "yh")
FEAT = ("yl", "z", "c")
NX, NZ = 4, 8

BLOCKS = (
    ((0, 0), (1, 0), (0, 1), (0, -1)),
    ((0, 2), (0, -2), (1, 1), (1, -1)),
    ((1, 2), (1, -2), (0, 3), (0, -3)),
    ((0, 4), (1, 3), (1, -3), (1, 4)),
)
SLOTS = tuple(slot for block in BLOCKS for slot in block)
PLACE = {slot: (b, k) for b, block in enumerate(BLOCKS) for k, slot in enumerate(block)}
OWN = (0, 0)


def own_tree(half, far):
    edges = {
        (0, 2): (OWN, "++"), (0, -2): (OWN, "--"), (1, 0): (OWN, "y"),
        (0, 1): (OWN, "+"), (0, -1): (OWN, "-"),
        (0, 3): ((0, 2), "+"), (0, -3): ((0, -2), "-"),
        (0, 4): ((0, 2), "++") if far == "+" else ((0, -2), "--"),
        (1, 1): ((1, 0), "+"), (1, -1): ((1, 0), "-"),
        (1, 2): ((0, 2), "y"), (1, -2): ((0, -2), "y"),
        (1, 3): ((0, 3), "y"), (1, -3): ((0, -3), "y"), (1, 4): ((0, 4), "y"),
    }
    return {(half, s): ((half, p), way) for s, (p, way) in edges.items()}


def next_tree():
    crossing = {(1, 2): (0, 2), (1, -2): (0, -2), (0, 0): (1, 0), (1, 0): (0, 0),
                (1, 1): (0, 1), (1, -1): (0, -1)}
    edges = {
        (1, 3): ((1, 2), "+"), (1, -3): ((1, -2), "-"), (1, 4): ((1, -2), "--"),
        (0, 1): ((0, 0), "+"), (0, -1): ((0, 0), "-"),
        (0, 2): ((0, 1), "+"), (0, -2): ((0, -1), "-"),
        (0, 3): ((1, 3), "y"), (0, -3): ((1, -3), "y"), (0, 4): ((1, 4), "y"),
    }
    return {(1, s): ((0, p), "cross") for s, p in crossing.items()} | {
        (1, s): ((1, p), way) for s, (p, way) in edges.items()
    }


INPUT_TREE = own_tree(0, "+") | own_tree(1, "-")
ERROR_TREE = next_tree() | own_tree(0, "+")
OWN_WAVES = (
    (OWN,),
    ((0, 2), (0, -2), (1, 0), (0, 1), (0, -1)),
    ((0, 3), (0, -3), (0, 4), (1, 1), (1, -1), (1, 2), (1, -2)),
    ((1, 3), (1, -3), (1, 4)),
)
NEXT_WAVES = (
    ((1, 0),),
    ((1, 2), (1, -2), (0, 0), (1, 1), (1, -1)),
    ((1, 3), (1, -3), (1, 4), (0, 1), (0, -1)),
    ((0, 3), (0, -3), (0, 4), (0, 2), (0, -2)),
)


def children_of(tree, node):
    return tuple(child for child, (parent, _) in tree.items() if parent == node)


def main_kernel(
    x_hbm, t_hbm, ew_hbm, eb_hbm, dw_hbm, db_hbm,
    tok_o, acts_o, grads_o, dpre_o, sums_o, loss_o,
    tok, ew, dw, eb, db, tg, pre, acts, part, sib_out, sib_in, arr, snd, zeros, gr, back, dpre, sums, squares, loss_all, loss_sum,
    load_sem, store_sem, tok_s, tok_r, tsib_s, tsib_r, psib_s, psib_r, red_s, red_r,
    gr_s, gr_r, gsib_s, gsib_r, loss_s, loss_r,
):
    x, yh = lax.axis_index("x"), lax.axis_index("yh")
    yl, z, c = lax.axis_index("yl"), lax.axis_index("z"), lax.axis_index("c")
    layer = x * 2 + yh
    width = dw.shape[2]
    half_width = width // 2

    to = {
        "+": {"z": lax.rem(z + 1, NZ)},
        "++": {"z": lax.rem(z + 2, NZ)},
        "-": {"z": lax.rem(z + NZ - 1, NZ)},
        "--": {"z": lax.rem(z + NZ - 2, NZ)},
        "y": {"yl": 1 - yl},
        "cross": {"x": lax.rem(x + yh + NX - 1, NX), "yh": 1 - yh, "yl": 1 - yl},
    }
    back_to = {
        "+": to["-"], "++": to["--"], "-": to["+"], "--": to["++"], "y": to["y"],
        "cross": {"x": lax.rem(x + yh, NX), "yh": 1 - yh, "yl": 1 - yl},
    }
    sibling = {"c": 1 - c}
    peers = [
        {"x": lax.rem(x + k // 2, NX), "yh": lax.rem(yh + k % 2, 2)} for k in range(1, 2 * NX)
    ]

    def load(k, src, dst):
        copy = pltpu.make_async_copy(src, dst, load_sem.at[k])
        copy.start()
        return copy

    zeros[...] = jnp.zeros_like(zeros)
    own_loads = [
        load(h, x_hbm.at[0, :, pl.ds(h * half_width, half_width)], tok.at[h, 0, 0, 0])
        for h in (0, 1)
    ]
    ew_load = load(2, ew_hbm.at[0], ew)
    eb_load = load(3, eb_hbm, eb)
    dw_loads = [load(4 + r, dw_hbm.at[0, r], dw.at[r]) for r in (1, 0)]
    tg_load = load(6, t_hbm.at[0], tg)
    db_load = load(7, db_hbm, db)

    barrier = pltpu.get_barrier_semaphore()
    greeted = [*to.values(), back_to["cross"], sibling, *peers]
    for device in greeted:
        pl.semaphore_signal(barrier, inc=1, device_id=device, device_id_type=MESH)
    pl.semaphore_wait(barrier, len(greeted))

    def remote(src, dst, send_sem, recv_sem, device):
        return pltpu.make_async_remote_copy(
            src_ref=src, dst_ref=dst, send_sem=send_sem, recv_sem=recv_sem,
            device_id=device, device_id_type=MESH,
        )

    sent = []

    def gather(tree, buf, ici_s, ici_r, sib_s, sib_r):
        ici, sib = {}, {}
        for h in (0, 1):
            for s in SLOTS:
                b, k = PLACE[s]
                sib[h, s] = remote(
                    buf.at[h, b, 0, k], buf.at[h, b, 1, k],
                    sib_s.at[h, b, k], sib_r.at[h, b, k], sibling,
                )

        def hop(node):
            (ph, parent), way = tree[node]
            h, s = node
            b, k = PLACE[s]
            pb, pk = PLACE[parent]
            sems = ici_s.at[h, b, k], ici_r.at[h, b, k]
            ici[node] = remote(buf.at[ph, pb, 0, pk], buf.at[h, b, 0, k], *sems, to[way])
            if way == "cross":
                blank = remote(zeros, buf.at[h, b, 0, k], *sems, to[way])
                pl.when(layer == 0)(blank.start)
                pl.when(layer != 0)(ici[node].start)
            else:
                ici[node].start()
            sent.append(ici[node])

        def stage(h, slots):
            for s in slots:
                if (h, s) in tree:
                    ici[h, s].wait_recv()
                for child in children_of(tree, (h, s)):
                    hop(child)
                sib[h, s].start()
                sent.append(sib[h, s])

        def settle(h, b):
            for s in BLOCKS[b]:
                sib[h, s].wait_recv()

        return stage, settle

    stage, settle = gather(INPUT_TREE, tok, tok_s, tok_r, tsib_s, tsib_r)

    def encode(b):
        rows = pl.ds(b * 128, 128)
        for h in (0, 1):
            settle(h, b)
        value = eb[...] + jnp.zeros((128, 1), F32)
        for h in (0, 1):
            value += jnp.dot(
                tok[h, b].reshape(128, half_width),
                ew[h * half_width : (h + 1) * half_width],
                preferred_element_type=F32,
            )
        value = jnp.maximum(value, 0.0)
        pre[rows] = value
        acts[rows] = (value * value).astype(BF16)

    for h in (0, 1):
        own_loads[h].wait()
        stage(h, OWN_WAVES[0])
    for h in (0, 1):
        stage(h, OWN_WAVES[1])
    ew_load.wait()
    eb_load.wait()
    encode(0)
    for h in (0, 1):
        stage(h, OWN_WAVES[2])
    encode(1)
    encode(2)
    for h in (0, 1):
        stage(h, OWN_WAVES[3])
    encode(3)
    stores = []

    def store(src, dst):
        copy = pltpu.make_async_copy(src, dst, store_sem.at[len(stores)])
        copy.start()
        stores.append(copy)

    store(tok, tok_o)
    store(acts, acts_o)

    psib = {
        (h, p): remote(
            sib_out.at[h, pl.ds(2 * p, 2)], sib_in.at[h, pl.ds(2 * p, 2)],
            psib_s.at[h, p], psib_r.at[h, p], sibling,
        )
        for h in (0, 1)
        for p in (0, 1)
    }
    tile = 512

    def decode(p):
        for h in (1, 0):

            @pl.loop(0, width // tile)
            def _(j):
                columns = pl.ds(pl.multiple_of(j * tile, tile), tile)
                value = jnp.dot(
                    acts[pl.ds(p * 256, 256)], dw[h, :, columns], preferred_element_type=F32
                ).reshape(2, 2, 4, 16, tile)
                for b in (0, 1):
                    part[h, 2 * p + b, :, :, columns] = value[b, 0]
                    sib_out[h, 2 * p + b, :, :, columns] = value[b, 1].astype(BF16)

            psib[h, p].start()
            sent.append(psib[h, p])

    red = {}
    for (h, s), (_, way) in ERROR_TREE.items():
        b, k = PLACE[s]
        red[h, s] = remote(
            snd.at[h, b, k], arr.at[h, b, k], red_s.at[h, b, k], red_r.at[h, b, k], back_to[way]
        )

    def total(h, s):
        b, k = PLACE[s]
        value = part[h, b, k] + sib_in[h, b, k].astype(F32)
        for child in children_of(ERROR_TREE, (h, s)):
            red[child].wait_recv()
            cb, ck = PLACE[child[1]]
            term = arr[child[0], cb, ck].astype(F32)
            if ERROR_TREE[child][1] == "cross":
                term = jnp.where(layer == 0, 0.0, term)
            value += term
        return value

    def pass_on(h, *slots):
        for s in slots:
            b, k = PLACE[s]
            snd[h, b, k] = total(h, s).astype(BF16)
            red[h, s].start()
            sent.append(red[h, s])

    for load_ in dw_loads:
        load_.wait()
    decode(1)
    psib[1, 1].wait_recv()
    pass_on(1, (0, 3), (0, -3), (0, 4))
    psib[0, 1].wait_recv()
    pass_on(0, (1, 3), (1, -3), (1, 4), (1, 2), (1, -2))
    decode(0)
    psib[1, 0].wait_recv()
    pass_on(1, (0, 2), (0, -2), (1, 3), (1, -3), (1, 4), (1, 1), (1, -1), (1, 0))
    psib[0, 0].wait_recv()
    pass_on(0, (1, 1), (1, -1), (0, 3), (0, -3), (0, 4))
    pass_on(1, (0, 1), (0, -1), (1, 2), (1, -2), (0, 0))
    tg_load.wait()
    db_load.wait()
    pass_on(0, (0, 1), (0, -1), (0, 2), (0, -2), (1, 0))
    gr[0, 0, 0, 0] = (total(0, OWN) + db[...] - tg[...].astype(F32)).astype(BF16)

    stage, settle = gather(ERROR_TREE, gr, gr_s, gr_r, gsib_s, gsib_r)

    def through(h):
        for b in range(4):
            settle(h, b)
        return lax.dot_general(
            gr[h].reshape(512, width), dw[h], (((1,), (1,)), ((), ())), preferred_element_type=F32
        )

    def add_up():
        @pl.loop(0, width // tile)
        def _(j):
            columns = pl.ds(pl.multiple_of(j * tile, tile), tile)
            total_sum = jnp.zeros((8, tile), F32)
            total_sq = jnp.zeros((8, tile), F32)
            for b in range(4):
                for p in range(2):
                    value = gr[0, b, p, :, :, columns].astype(F32).reshape(8, 8, tile)
                    total_sum += jnp.sum(value, axis=0)
                    total_sq += jnp.sum(value * value, axis=0)
            sums[:, columns] = total_sum
            squares[:, columns] = total_sq

        value = jnp.zeros((8, 128), F32)
        for j in range(width // 128):
            value += squares[:, j * 128 : (j + 1) * 128]
        loss_all[0] = value
        store(sums, sums_o)

    stage(0, OWN_WAVES[0])
    stage(0, OWN_WAVES[1])
    stage(1, NEXT_WAVES[0])
    stage(0, OWN_WAVES[2])
    stage(1, NEXT_WAVES[1])
    stage(0, OWN_WAVES[3])
    stage(1, NEXT_WAVES[2])
    back[...] = through(0)
    add_up()
    tells = []
    for k, device in enumerate(peers):
        tells.append(
            remote(loss_all.at[0], loss_all.at[k + 1], loss_s.at[k], loss_r.at[k], device)
        )
        tells[-1].start()
    store(gr.at[0], grads_o.at[0])
    stage(1, NEXT_WAVES[3])
    dpre[...] = ((through(1) + back[...]) * 2.0 * pre[...]).astype(BF16)
    store(gr.at[1], grads_o.at[1])
    store(dpre, dpre_o)
    for tell in tells:
        tell.wait_recv()
    sent += tells
    value = loss_all[0]
    for k in range(1, 2 * NX):
        value += loss_all[k]
    loss_sum[...] = value
    store(loss_sum, loss_o)
    for copy in sent:
        copy.wait_send()
    for copy in stores:
        copy.wait()


def grad_kernel(scale, tok, acts, dpre, grads, sums, loss, eg, ebg, dg, dbg, mean):
    contract = (((0,), (0,)), ((), ()))
    eg[0] = lax.dot_general(tok[0], dpre[...], contract, preferred_element_type=F32).astype(BF16)
    for r in (0, 1):
        dg[0, r] = lax.dot_general(
            acts[...], grads[r], contract, preferred_element_type=F32
        ).astype(BF16)

    @pl.when(pl.program_id(0) == 0)
    def _():
        ebg[...] = jnp.sum(dpre[...].astype(F32), axis=0, keepdims=True)
        dbg[...] = jnp.sum(sums[...], axis=0, keepdims=True)
        mean[0, 0] = jnp.sum(loss[...]) * scale


def shards(inputs, targets, enc_weight, enc_bias, dec_weight, dec_bias):
    rows, width = inputs.shape[1:]
    feats = enc_weight.shape[2]
    tokens = rows * 32
    half_width = width // 2
    anywhere = pl.BlockSpec(memory_space=pl.ANY)
    dma = pltpu.SemaphoreType.DMA
    tok, acts, grads, dpre, sums, loss = pl.pallas_call(
        main_kernel,
        out_shape=(
            jax.ShapeDtypeStruct((2, 4, 2, 4, rows, half_width), BF16),
            jax.ShapeDtypeStruct((tokens, feats), BF16),
            jax.ShapeDtypeStruct((2, 4, 2, 4, rows, width), BF16),
            jax.ShapeDtypeStruct((tokens, feats), BF16),
            jax.ShapeDtypeStruct((8, width), F32),
            jax.ShapeDtypeStruct((8, 128), F32),
        ),
        in_specs=[anywhere] * 6,
        out_specs=(anywhere,) * 6,
        scratch_shapes=[
            pltpu.VMEM((2, 4, 2, 4, rows, half_width), BF16),
            pltpu.VMEM((width, feats), BF16),
            pltpu.VMEM((2, feats, width), BF16),
            pltpu.VMEM((1, feats), F32),
            pltpu.VMEM((1, width), F32),
            pltpu.VMEM((rows, width), BF16),
            pltpu.VMEM((tokens, feats), F32),
            pltpu.VMEM((tokens, feats), BF16),
            pltpu.VMEM((2, 4, 4, rows, width), F32),
            pltpu.VMEM((2, 4, 4, rows, width), BF16),
            pltpu.VMEM((2, 4, 4, rows, width), BF16),
            pltpu.VMEM((2, 4, 4, rows, width), BF16),
            pltpu.VMEM((2, 4, 4, rows, width), BF16),
            pltpu.VMEM((rows, width), BF16),
            pltpu.VMEM((2, 4, 2, 4, rows, width), BF16),
            pltpu.VMEM((tokens, feats), F32),
            pltpu.VMEM((tokens, feats), BF16),
            pltpu.VMEM((8, width), F32),
            pltpu.VMEM((8, width), F32),
            pltpu.VMEM((2 * NX, 8, 128), F32),
            pltpu.VMEM((8, 128), F32),
            dma((8,)),
            dma((8,)),
            *[dma((2, 4, 4))] * 4,
            *[dma((2, 2))] * 2,
            *[dma((2, 4, 4))] * 2,
            *[dma((2, 4, 4))] * 4,
            *[dma((2 * NX - 1,))] * 2,
        ],
        compiler_params=pltpu.CompilerParams(
            collective_id=0, has_side_effects=True, vmem_limit_bytes=60 * 2**20
        ),
        name="exchange",
    )(inputs, targets, enc_weight, enc_bias, dec_weight, dec_bias)
    tok = tok.reshape(2, tokens, half_width)
    grads = grads.reshape(2, tokens, width)
    whole = lambda *shape: pl.BlockSpec(shape, lambda i: (0,) * len(shape))
    eg, ebg, dg, dbg, mean = pl.pallas_call(
        lambda *refs: grad_kernel(1.0 / (2 * NX * tokens * width), *refs),
        grid=(4,),
        out_shape=(
            jax.ShapeDtypeStruct((1, width, feats), BF16),
            jax.ShapeDtypeStruct((1, feats), F32),
            jax.ShapeDtypeStruct((1, 2, feats, width), BF16),
            jax.ShapeDtypeStruct((1, width), F32),
            jax.ShapeDtypeStruct((1, 1), F32),
        ),
        in_specs=[
            pl.BlockSpec((1, tokens, width // 4), lambda i: (i // 2, 0, i % 2)),
            whole(tokens, feats),
            whole(tokens, feats),
            pl.BlockSpec((2, tokens, width // 4), lambda i: (0, 0, i)),
            whole(8, width),
            whole(8, 128),
        ],
        out_specs=(
            pl.BlockSpec((1, width // 4, feats), lambda i: (0, i, 0)),
            whole(1, feats),
            pl.BlockSpec((1, 2, feats, width // 4), lambda i: (0, 0, 0, i)),
            whole(1, width),
            pl.BlockSpec(memory_space=pltpu.SMEM),
        ),
        name="weight_grads",
    )(tok, acts, dpre, grads, sums, loss)
    return mean[0, 0], eg, ebg, dg, dbg


def solution(mesh):
    finer = Mesh(mesh.devices.reshape(NX, 2, 2, NZ, 2), LAYER + FEAT)
    return jax.shard_map(
        shards,
        mesh=finer,
        in_specs=(
            P(LAYER, FEAT, None),
            P(LAYER, FEAT, None),
            P(LAYER, None, FEAT),
            P(LAYER, FEAT),
            P(LAYER, None, FEAT, None),
            P(LAYER, None),
        ),
        out_specs=(
            P(),
            P(LAYER, None, FEAT),
            P(LAYER, FEAT),
            P(LAYER, None, FEAT, None),
            P(LAYER, None),
        ),
        check_vma=False,
    )
```

time: 105 us -> 90.4 us (0.86); the launches traced: 103 us -> 90.1 us
  Pallas kernels: 102 us -> 89.5 us
    pallas_call x1, Pallas kernels: 92.2 us -> 81.2 us  [shards(): pl.pallas_call(main_kernel, out_shape=(jax.ShapeDtypeStruct((2, 4, 2, 4,...]
    pallas_call x1, Pallas kernels: 10.1 us -> 8.26 us  [shards(): pl.pallas_call(lambda *refs: grad_kernel(1.0 / (2 * NX * tokens * width),...]
where the time goes in v2:
time: 90.4 us; the launch traced here: 90.1 us
  Pallas kernels  89.5 us (99%)
    pallas_call x1, Pallas kernels, shards(): pl.pallas_call(main_kernel, out_shape=(jax.ShapeDtypeStruct((2, 4, 2, 4,...  81.2 us
    pallas_call x1, Pallas kernels, shards(): pl.pallas_call(lambda *refs: grad_kernel(1.0 / (2 * NX * tokens * width),...  8.26 us

profile of v2, /device:TPU:1, one launch (start us, length us, event | category | flops | bytes accessed | tf_op | source)
XLA Modules:
  0.0 90.1 jit_solution(5157794040171250393)
XLA Ops:
  0.6 81.2 %exchange.1 = (bf16[2,4,2,4,16,1024]{5,4,3,2,1,0:T(8,128)(2,1)}, bf16[512,512]{1,0:T(8,128)(2,1)}, bf16[2,4,2,4,16,2048]{5,4,3,2,1,0:T(8,128)(2,1)}, bf16[512,51...) custom-call(bf16[1,16,2048]{2,1,0:T(8,128)(2,1)} %x_hbm.1, bf16[1,16,2048]{2,1,0:T(8,128)(2,1)} %t_hbm.1, ...), custom_call_target="tpu_custom_call" | custom-call | tf_op jit(solution)/shard_map/exchange/pallas_call | solution.py:370
  81.9 8.3 %weight_grads.1 = (bf16[1,2048,512]{2,1,0:T(8,128)(2,1)}, f32[1,512]{1,0:T(1,128)}, bf16[1,2,512,2048]{3,2,1,0:T(8,128)(2,1)}, f32[1,2048]{1,0:T(1,128)}, f32[1,1]{1,0:T(1,128)}) custom-call(bf16[2,512,1024]{2,1,0:T(8,128)(2,1)} %bitcast.4, bf16[512,512]{1,0:T(8,128)(2,1)} %get-tuple-element.17.refs_1_, bf16[512,512]{1,0:T(8,128)(2,1)} %get-tuple-element.18.refs_2_, ...), custom_call_target="tpu_custom_call" | custom-call | tf_op jit(solution)/shard_map/weight_grads/pallas_call | solution.py:420

commit v3 on v2

--- a/solution.py
+++ b/solution.py
@@ -15,8 +15,8 @@
 BLOCKS = (
     ((0, 0), (1, 0), (0, 1), (0, -1)),
     ((0, 2), (0, -2), (1, 1), (1, -1)),
-    ((1, 2), (1, -2), (0, 3), (0, -3)),
-    ((0, 4), (1, 3), (1, -3), (1, 4)),
+    ((1, 2), (1, -2), (1, 3), (1, -3)),
+    ((0, 4), (0, 3), (0, -3), (1, 4)),
 )
 SLOTS = tuple(slot for block in BLOCKS for slot in block)
 PLACE = {slot: (b, k) for b, block in enumerate(BLOCKS) for k, slot in enumerate(block)}
@@ -37,15 +37,13 @@
 
 
 def next_tree():
-    crossing = {(1, 2): (0, 2), (1, -2): (0, -2), (0, 0): (1, 0), (1, 0): (0, 0),
-                (1, 1): (0, 1), (1, -1): (0, -1)}
+    crossing = ((1, 2), (1, -2), (0, 0), (1, 0), (1, 1), (1, -1), (0, 2), (0, -2))
     edges = {
         (1, 3): ((1, 2), "+"), (1, -3): ((1, -2), "-"), (1, 4): ((1, -2), "--"),
         (0, 1): ((0, 0), "+"), (0, -1): ((0, 0), "-"),
-        (0, 2): ((0, 1), "+"), (0, -2): ((0, -1), "-"),
         (0, 3): ((1, 3), "y"), (0, -3): ((1, -3), "y"), (0, 4): ((1, 4), "y"),
     }
-    return {(1, s): ((0, p), "cross") for s, p in crossing.items()} | {
+    return {(1, (dy, dz)): ((0, (1 - dy, dz)), "cross") for dy, dz in crossing} | {
         (1, s): ((1, p), way) for s, (p, way) in edges.items()
     }
 
@@ -61,8 +59,8 @@
 NEXT_WAVES = (
     ((1, 0),),
     ((1, 2), (1, -2), (0, 0), (1, 1), (1, -1)),
-    ((1, 3), (1, -3), (1, 4), (0, 1), (0, -1)),
-    ((0, 3), (0, -3), (0, 4), (0, 2), (0, -2)),
+    ((1, 3), (1, -3), (1, 4), (0, 1), (0, -1), (0, 2), (0, -2)),
+    ((0, 3), (0, -3), (0, 4)),
 )
 
 
@@ -72,9 +70,10 @@
 
 def main_kernel(
     x_hbm, t_hbm, ew_hbm, eb_hbm, dw_hbm, db_hbm,
-    tok_o, acts_o, grads_o, dpre_o, sums_o, loss_o,
-    tok, ew, dw, eb, db, tg, pre, acts, part, sib_out, sib_in, arr, snd, zeros, gr, back, dpre, sums, squares, loss_all, loss_sum,
-    load_sem, store_sem, tok_s, tok_r, tsib_s, tsib_r, psib_s, psib_r, red_s, red_r,
+    tok, acts, gr1, dpre, dg0, sums, loss_sum,
+    ew, dw, eb, db, tg, pre, part, sib_out, sib_in, arr, snd, zeros, gr0, back, dg_sum,
+    squares, loss_all,
+    load_sem, tok_s, tok_r, tsib_s, tsib_r, psib_s, psib_r, red_s, red_r,
     gr_s, gr_r, gsib_s, gsib_r, loss_s, loss_r,
 ):
     x, yh = lax.axis_index("x"), lax.axis_index("yh")
@@ -136,7 +135,7 @@
             for s in SLOTS:
                 b, k = PLACE[s]
                 sib[h, s] = remote(
-                    buf.at[h, b, 0, k], buf.at[h, b, 1, k],
+                    buf[h].at[b, 0, k], buf[h].at[b, 1, k],
                     sib_s.at[h, b, k], sib_r.at[h, b, k], sibling,
                 )
 
@@ -146,9 +145,9 @@
             b, k = PLACE[s]
             pb, pk = PLACE[parent]
             sems = ici_s.at[h, b, k], ici_r.at[h, b, k]
-            ici[node] = remote(buf.at[ph, pb, 0, pk], buf.at[h, b, 0, k], *sems, to[way])
+            ici[node] = remote(buf[ph].at[pb, 0, pk], buf[h].at[b, 0, k], *sems, to[way])
             if way == "cross":
-                blank = remote(zeros, buf.at[h, b, 0, k], *sems, to[way])
+                blank = remote(zeros, buf[h].at[b, 0, k], *sems, to[way])
                 pl.when(layer == 0)(blank.start)
                 pl.when(layer != 0)(ici[node].start)
             else:
@@ -170,47 +169,23 @@
 
         return stage, settle
 
-    stage, settle = gather(INPUT_TREE, tok, tok_s, tok_r, tsib_s, tsib_r)
-
-    def encode(b):
-        rows = pl.ds(b * 128, 128)
+    stage, settle = gather(INPUT_TREE, (tok.at[0], tok.at[1]), tok_s, tok_r, tsib_s, tsib_r)
+
+    def encode(first, blocks):
+        rows = pl.ds(first * 128, blocks * 128)
         for h in (0, 1):
-            settle(h, b)
-        value = eb[...] + jnp.zeros((128, 1), F32)
+            for b in range(first, first + blocks):
+                settle(h, b)
+        value = eb[...] + jnp.zeros((blocks * 128, 1), F32)
         for h in (0, 1):
             value += jnp.dot(
-                tok[h, b].reshape(128, half_width),
+                tok[h, first : first + blocks].reshape(blocks * 128, half_width),
                 ew[h * half_width : (h + 1) * half_width],
                 preferred_element_type=F32,
             )
         value = jnp.maximum(value, 0.0)
         pre[rows] = value
         acts[rows] = (value * value).astype(BF16)
-
-    for h in (0, 1):
-        own_loads[h].wait()
-        stage(h, OWN_WAVES[0])
-    for h in (0, 1):
-        stage(h, OWN_WAVES[1])
-    ew_load.wait()
-    eb_load.wait()
-    encode(0)
-    for h in (0, 1):
-        stage(h, OWN_WAVES[2])
-    encode(1)
-    encode(2)
-    for h in (0, 1):
-        stage(h, OWN_WAVES[3])
-    encode(3)
-    stores = []
-
-    def store(src, dst):
-        copy = pltpu.make_async_copy(src, dst, store_sem.at[len(stores)])
-        copy.start()
-        stores.append(copy)
-
-    store(tok, tok_o)
-    store(acts, acts_o)
 
     psib = {
         (h, p): remote(
@@ -264,32 +239,70 @@
             red[h, s].start()
             sent.append(red[h, s])
 
+    for h in (0, 1):
+        own_loads[h].wait()
+        stage(h, OWN_WAVES[0])
+    for h in (0, 1):
+        stage(h, OWN_WAVES[1])
+    ew_load.wait()
+    eb_load.wait()
+    for h in (0, 1):
+        stage(h, OWN_WAVES[2])
+    encode(0, 2)
     for load_ in dw_loads:
         load_.wait()
+    decode(0)
+    for h in (0, 1):
+        stage(h, OWN_WAVES[3])
+    psib[1, 0].wait_recv()
+    pass_on(1, (0, 2), (0, -2), (0, 1), (0, -1), (1, 1), (1, -1), (1, 0))
+    psib[0, 0].wait_recv()
+    pass_on(0, (1, 1), (1, -1))
+    encode(2, 2)
     decode(1)
+    pass_on(1, (0, 0))
     psib[1, 1].wait_recv()
     pass_on(1, (0, 3), (0, -3), (0, 4))
     psib[0, 1].wait_recv()
     pass_on(0, (1, 3), (1, -3), (1, 4), (1, 2), (1, -2))
-    decode(0)
-    psib[1, 0].wait_recv()
-    pass_on(1, (0, 2), (0, -2), (1, 3), (1, -3), (1, 4), (1, 1), (1, -1), (1, 0))
-    psib[0, 0].wait_recv()
-    pass_on(0, (1, 1), (1, -1), (0, 3), (0, -3), (0, 4))
-    pass_on(1, (0, 1), (0, -1), (1, 2), (1, -2), (0, 0))
+    pass_on(1, (1, 3), (1, -3), (1, 4))
+    pass_on(0, (0, 3), (0, -3), (0, 4))
+    pass_on(0, (0, 1), (0, -1), (1, 0))
+    pass_on(1, (1, 2), (1, -2))
     tg_load.wait()
     db_load.wait()
-    pass_on(0, (0, 1), (0, -1), (0, 2), (0, -2), (1, 0))
-    gr[0, 0, 0, 0] = (total(0, OWN) + db[...] - tg[...].astype(F32)).astype(BF16)
-
-    stage, settle = gather(ERROR_TREE, gr, gr_s, gr_r, gsib_s, gsib_r)
-
-    def through(h):
-        for b in range(4):
+    pass_on(0, (0, 2), (0, -2))
+    gr0[0, 0, 0] = (total(0, OWN) + db[...] - tg[...].astype(F32)).astype(BF16)
+
+    stage, settle = gather(ERROR_TREE, (gr0, gr1), gr_s, gr_r, gsib_s, gsib_r)
+    gr = (gr0, gr1)
+
+    def through(h, first, blocks):
+        rows = pl.ds(first * 128, blocks * 128)
+        for b in range(first, first + blocks):
             settle(h, b)
-        return lax.dot_general(
-            gr[h].reshape(512, width), dw[h], (((1,), (1,)), ((), ())), preferred_element_type=F32
+        value = lax.dot_general(
+            gr[h][first : first + blocks].reshape(blocks * 128, width), dw[h],
+            (((1,), (1,)), ((), ())), preferred_element_type=F32,
         )
+        if h == 0:
+            back[rows] = value
+        else:
+            dpre[rows] = ((value + back[rows]) * 2.0 * pre[rows]).astype(BF16)
+
+    def decoder_grad(p):
+        @pl.loop(0, width // tile)
+        def _(j):
+            columns = pl.ds(pl.multiple_of(j * tile, tile), tile)
+            value = lax.dot_general(
+                acts[pl.ds(p * 256, 256)],
+                gr0[2 * p : 2 * p + 2, :, :, :, columns].reshape(256, tile),
+                (((0,), (0,)), ((), ())), preferred_element_type=F32,
+            )
+            if p == 0:
+                dg_sum[:, columns] = value
+            else:
+                dg0[:, columns] = (value + dg_sum[:, columns]).astype(BF16)
 
     def add_up():
         @pl.loop(0, width // tile)
@@ -299,7 +312,7 @@
             total_sq = jnp.zeros((8, tile), F32)
             for b in range(4):
                 for p in range(2):
-                    value = gr[0, b, p, :, :, columns].astype(F32).reshape(8, 8, tile)
+                    value = gr0[b, p, :, :, columns].astype(F32).reshape(8, 8, tile)
                     total_sum += jnp.sum(value, axis=0)
                     total_sq += jnp.sum(value * value, axis=0)
             sums[:, columns] = total_sum
@@ -309,16 +322,17 @@
         for j in range(width // 128):
             value += squares[:, j * 128 : (j + 1) * 128]
         loss_all[0] = value
-        store(sums, sums_o)
 
     stage(0, OWN_WAVES[0])
     stage(0, OWN_WAVES[1])
     stage(1, NEXT_WAVES[0])
     stage(0, OWN_WAVES[2])
     stage(1, NEXT_WAVES[1])
+    through(0, 0, 2)
+    decoder_grad(0)
     stage(0, OWN_WAVES[3])
     stage(1, NEXT_WAVES[2])
-    back[...] = through(0)
+    through(0, 2, 2)
     add_up()
     tells = []
     for k, device in enumerate(peers):
@@ -326,11 +340,10 @@
             remote(loss_all.at[0], loss_all.at[k + 1], loss_s.at[k], loss_r.at[k], device)
         )
         tells[-1].start()
-    store(gr.at[0], grads_o.at[0])
+    decoder_grad(1)
     stage(1, NEXT_WAVES[3])
-    dpre[...] = ((through(1) + back[...]) * 2.0 * pre[...]).astype(BF16)
-    store(gr.at[1], grads_o.at[1])
-    store(dpre, dpre_o)
+    through(1, 0, 3)
+    through(1, 3, 1)
     for tell in tells:
         tell.wait_recv()
     sent += tells
@@ -338,26 +351,42 @@
     for k in range(1, 2 * NX):
         value += loss_all[k]
     loss_sum[...] = value
-    store(loss_sum, loss_o)
     for copy in sent:
         copy.wait_send()
-    for copy in stores:
+
+
+def grad_kernel(
+    scale, tok, acts, gr1, dpre, dg0, sums, loss, eg_o, ebg_o, dg_o, dbg_o, mean,
+    eg, dg, ebg, dbg, sems,
+):
+    contract = (((0,), (0,)), ((), ()))
+    copies = []
+
+    def store(src, dst):
+        copies.append(pltpu.make_async_copy(src, dst, sems.at[len(copies)]))
+        copies[-1].start()
+
+    store(dg0, dg_o.at[0, 0])
+    tokens, half_width = tok.shape[1:]
+    tile = 512
+    for j in range(2 * half_width // tile):
+        at = j * tile
+        part = tok[at // half_width, :, at % half_width : at % half_width + tile]
+        eg[j] = lax.dot_general(part, dpre[...], contract, preferred_element_type=F32).astype(BF16)
+        store(eg.at[j], eg_o.at[0, pl.ds(at, tile)])
+    ebg[...] = jnp.sum(dpre[...].astype(F32), axis=0, keepdims=True)
+    dbg[...] = jnp.sum(sums[...], axis=0, keepdims=True)
+    store(ebg, ebg_o)
+    store(dbg, dbg_o)
+    for j in range(gr1.shape[1] // tile):
+        at = j * tile
+        dg[j] = lax.dot_general(
+            acts[...], gr1[:, at : at + tile], contract, preferred_element_type=F32
+        ).astype(BF16)
+        store(dg.at[j], dg_o.at[0, 1, :, pl.ds(at, tile)])
+    mean[0, 0] = jnp.sum(loss[...]) * scale
+    for copy in copies:
         copy.wait()
-
-
-def grad_kernel(scale, tok, acts, dpre, grads, sums, loss, eg, ebg, dg, dbg, mean):
-    contract = (((0,), (0,)), ((), ()))
-    eg[0] = lax.dot_general(tok[0], dpre[...], contract, preferred_element_type=F32).astype(BF16)
-    for r in (0, 1):
-        dg[0, r] = lax.dot_general(
-            acts[...], grads[r], contract, preferred_element_type=F32
-        ).astype(BF16)
-
-    @pl.when(pl.program_id(0) == 0)
-    def _():
-        ebg[...] = jnp.sum(dpre[...].astype(F32), axis=0, keepdims=True)
-        dbg[...] = jnp.sum(sums[...], axis=0, keepdims=True)
-        mean[0, 0] = jnp.sum(loss[...]) * scale
 
 
 def shards(inputs, targets, enc_weight, enc_bias, dec_weight, dec_bias):
@@ -366,42 +395,40 @@
     tokens = rows * 32
     half_width = width // 2
     anywhere = pl.BlockSpec(memory_space=pl.ANY)
+    here = pl.BlockSpec(memory_space=pltpu.VMEM)
     dma = pltpu.SemaphoreType.DMA
-    tok, acts, grads, dpre, sums, loss = pl.pallas_call(
+    chunks = (4, 2, 4, rows)
+    tok, acts, gr1, dpre, dg0, sums, loss = pl.pallas_call(
         main_kernel,
         out_shape=(
-            jax.ShapeDtypeStruct((2, 4, 2, 4, rows, half_width), BF16),
-            jax.ShapeDtypeStruct((tokens, feats), BF16),
-            jax.ShapeDtypeStruct((2, 4, 2, 4, rows, width), BF16),
-            jax.ShapeDtypeStruct((tokens, feats), BF16),
-            jax.ShapeDtypeStruct((8, width), F32),
-            jax.ShapeDtypeStruct((8, 128), F32),
+            pltpu.VMEM((2, *chunks, half_width), BF16),
+            pltpu.VMEM((tokens, feats), BF16),
+            pltpu.VMEM((*chunks, width), BF16),
+            pltpu.VMEM((tokens, feats), BF16),
+            pltpu.VMEM((feats, width), BF16),
+            pltpu.VMEM((8, width), F32),
+            pltpu.VMEM((8, 128), F32),
         ),
         in_specs=[anywhere] * 6,
-        out_specs=(anywhere,) * 6,
+        out_specs=(here,) * 7,
         scratch_shapes=[
-            pltpu.VMEM((2, 4, 2, 4, rows, half_width), BF16),
             pltpu.VMEM((width, feats), BF16),
             pltpu.VMEM((2, feats, width), BF16),
             pltpu.VMEM((1, feats), F32),
             pltpu.VMEM((1, width), F32),
             pltpu.VMEM((rows, width), BF16),
             pltpu.VMEM((tokens, feats), F32),
-            pltpu.VMEM((tokens, feats), BF16),
             pltpu.VMEM((2, 4, 4, rows, width), F32),
             pltpu.VMEM((2, 4, 4, rows, width), BF16),
             pltpu.VMEM((2, 4, 4, rows, width), BF16),
             pltpu.VMEM((2, 4, 4, rows, width), BF16),
             pltpu.VMEM((2, 4, 4, rows, width), BF16),
             pltpu.VMEM((rows, width), BF16),
-            pltpu.VMEM((2, 4, 2, 4, rows, width), BF16),
+            pltpu.VMEM((*chunks, width), BF16),
             pltpu.VMEM((tokens, feats), F32),
-            pltpu.VMEM((tokens, feats), BF16),
-            pltpu.VMEM((8, width), F32),
+            pltpu.VMEM((feats, width), F32),
             pltpu.VMEM((8, width), F32),
             pltpu.VMEM((2 * NX, 8, 128), F32),
-            pltpu.VMEM((8, 128), F32),
-            dma((8,)),
             dma((8,)),
             *[dma((2, 4, 4))] * 4,
             *[dma((2, 2))] * 2,
@@ -410,16 +437,15 @@
             *[dma((2 * NX - 1,))] * 2,
         ],
         compiler_params=pltpu.CompilerParams(
-            collective_id=0, has_side_effects=True, vmem_limit_bytes=60 * 2**20
+            collective_id=0, has_side_effects=True, vmem_limit_bytes=50 * 2**20
         ),
         name="exchange",
     )(inputs, targets, enc_weight, enc_bias, dec_weight, dec_bias)
     tok = tok.reshape(2, tokens, half_width)
-    grads = grads.reshape(2, tokens, width)
-    whole = lambda *shape: pl.BlockSpec(shape, lambda i: (0,) * len(shape))
+    gr1 = gr1.reshape(tokens, width)
+    scale = 1.0 / (2 * NX * tokens * width)
     eg, ebg, dg, dbg, mean = pl.pallas_call(
-        lambda *refs: grad_kernel(1.0 / (2 * NX * tokens * width), *refs),
-        grid=(4,),
+        lambda *refs: grad_kernel(scale, *refs),
         out_shape=(
             jax.ShapeDtypeStruct((1, width, feats), BF16),
             jax.ShapeDtypeStruct((1, feats), F32),
@@ -427,23 +453,18 @@
             jax.ShapeDtypeStruct((1, width), F32),
             jax.ShapeDtypeStruct((1, 1), F32),
         ),
-        in_specs=[
-            pl.BlockSpec((1, tokens, width // 4), lambda i: (i // 2, 0, i % 2)),
-            whole(tokens, feats),
-            whole(tokens, feats),
-            pl.BlockSpec((2, tokens, width // 4), lambda i: (0, 0, i)),
-            whole(8, width),
-            whole(8, 128),
+        in_specs=[here] * 7,
+        out_specs=(*[anywhere] * 4, pl.BlockSpec(memory_space=pltpu.SMEM)),
+        scratch_shapes=[
+            pltpu.VMEM((width // 512, 512, feats), BF16),
+            pltpu.VMEM((width // 512, feats, 512), BF16),
+            pltpu.VMEM((1, feats), F32),
+            pltpu.VMEM((1, width), F32),
+            dma((3 + 2 * (width // 512),)),
         ],
-        out_specs=(
-            pl.BlockSpec((1, width // 4, feats), lambda i: (0, i, 0)),
-            whole(1, feats),
-            pl.BlockSpec((1, 2, feats, width // 4), lambda i: (0, 0, 0, i)),
-            whole(1, width),
-            pl.BlockSpec(memory_space=pltpu.SMEM),
-        ),
+        compiler_params=pltpu.CompilerParams(vmem_limit_bytes=24 * 2**20),
         name="weight_grads",
-    )(tok, acts, dpre, grads, sums, loss)
+    )(tok, acts, gr1, dpre, dg0, sums, loss)
     return mean[0, 0], eg, ebg, dg, dbg
 
 

time: 90.4 us -> 83.9 us (0.928)
  Pallas kernels: 89.5 us -> 83.2 us
    pallas_call x2, Pallas kernels: 89.5 us -> 83.2 us  [the longest x1 79.4 us: shards(): pl.pallas_call(main_kernel, out_shape=(pltpu.VMEM((2, *chunks, half_width...]
where the time goes in v3:
time: 83.9 us; the launch traced here: 83.8 us
  Pallas kernels  83.2 us (99%)
    pallas_call x1, Pallas kernels, shards(): pl.pallas_call(main_kernel, out_shape=(pltpu.VMEM((2, *chunks, half_width...  79.4 us
    pallas_call x1, Pallas kernels, shards(): pl.pallas_call(lambda *refs: grad_kernel(scale, *refs), out_shape=(jax.Sh...  3.8 us

profile of v3, /device:TPU:1, one launch (start us, length us, event | category | flops | bytes accessed | tf_op | source)
XLA Modules:
  0.0 83.8 jit_solution(3344219418715622195)
XLA Ops:
  0.6 79.4 %exchange.1 = (bf16[2,4,2,4,16,1024]{5,4,3,2,1,0:T(8,128)(2,1)S(1)}, bf16[512,512]{1,0:T(8,128)(2,1)S(1)}, bf16[4,2,4,16,2048]{4,3,2,1,0:T(8,128)(2,1)S(1)}, bf1...) custom-call(bf16[1,16,2048]{2,1,0:T(8,128)(2,1)} %x_hbm.1, ...), custom_call_target="tpu_custom_call" | custom-call | tf_op jit(solution)/shard_map/exchange/pallas_call | solution.py:401
  80.0 3.8 %weight_grads.1 = (bf16[1,2048,512]{2,1,0:T(8,128)(2,1)}, f32[1,512]{1,0:T(1,128)}, bf16[1,2,512,2048]{3,2,1,0:T(8,128)(2,1)}, f32[1,2048]{1,0:T(1,128)}, f32[1,1]{1,0:T(1,128)}) custom-call(bf16[2,512,1024]{2,1,0:T(8,128)(2,1)S(1)} %bitcast.3, bf16[512,512]{1,0:T(8,128)(2,1)S(1)} %get-tuple-element.18.refs_1_, bf16[512,2048]{1,0:T(8,128)(2,1)S(1)} %bitcast.4, ...), custom_call_target="tpu_custom_call" | custom-call | tf_op jit(solution)/shard_map/weight_grads/pallas_call | solution.py:447

commit v4 on v3

--- a/solution.py
+++ b/solution.py
@@ -36,10 +36,11 @@
     return {(half, s): ((half, p), way) for s, (p, way) in edges.items()}
 
 
-def next_tree():
+def next_tree(far):
     crossing = ((1, 2), (1, -2), (0, 0), (1, 0), (1, 1), (1, -1), (0, 2), (0, -2))
     edges = {
-        (1, 3): ((1, 2), "+"), (1, -3): ((1, -2), "-"), (1, 4): ((1, -2), "--"),
+        (1, 3): ((1, 2), "+"), (1, -3): ((1, -2), "-"),
+        (1, 4): ((1, 2), "++") if far == "+" else ((1, -2), "--"),
         (0, 1): ((0, 0), "+"), (0, -1): ((0, 0), "-"),
         (0, 3): ((1, 3), "y"), (0, -3): ((1, -3), "y"), (0, 4): ((1, 4), "y"),
     }
@@ -49,7 +50,7 @@
 
 
 INPUT_TREE = own_tree(0, "+") | own_tree(1, "-")
-ERROR_TREE = next_tree() | own_tree(0, "+")
+ERROR_TREES = (next_tree("-") | own_tree(0, "+"), next_tree("+") | own_tree(0, "-"))
 OWN_WAVES = (
     (OWN,),
     ((0, 2), (0, -2), (1, 0), (0, 1), (0, -1)),
@@ -71,9 +72,9 @@
 def main_kernel(
     x_hbm, t_hbm, ew_hbm, eb_hbm, dw_hbm, db_hbm,
     tok, acts, gr1, dpre, dg0, sums, loss_sum,
-    ew, dw, eb, db, tg, pre, part, sib_out, sib_in, arr, snd, zeros, gr0, back, dg_sum,
+    ew, dw, eb, ew2, dw2, eb2, db, tg, pre, acts2, part, arr, snd, zeros, gr0, back, dg_sum,
     squares, loss_all,
-    load_sem, tok_s, tok_r, tsib_s, tsib_r, psib_s, psib_r, red_s, red_r,
+    load_sem, tok_s, tok_r, tsib_s, tsib_r, copy_s, copy_r, red_s, red_r,
     gr_s, gr_r, gsib_s, gsib_r, loss_s, loss_r,
 ):
     x, yh = lax.axis_index("x"), lax.axis_index("yh")
@@ -158,7 +159,11 @@
             for s in slots:
                 if (h, s) in tree:
                     ici[h, s].wait_recv()
+                late = [n for n in children_of(tree, (h, s)) if not children_of(tree, n)]
                 for child in children_of(tree, (h, s)):
+                    if child not in late:
+                        hop(child)
+                for child in late:
                     hop(child)
                 sib[h, s].start()
                 sent.append(sib[h, s])
@@ -171,167 +176,233 @@
 
     stage, settle = gather(INPUT_TREE, (tok.at[0], tok.at[1]), tok_s, tok_r, tsib_s, tsib_r)
 
-    def encode(first, blocks):
-        rows = pl.ds(first * 128, blocks * 128)
-        for h in (0, 1):
-            for b in range(first, first + blocks):
-                settle(h, b)
-        value = eb[...] + jnp.zeros((blocks * 128, 1), F32)
+    copies = [
+        remote(src, dst, copy_s.at[k], copy_r.at[k], sibling)
+        for k, (src, dst) in enumerate(
+            ((ew_hbm.at[0], ew2), (eb_hbm, eb2), (dw_hbm.at[0, 1], dw2.at[1]), (dw_hbm.at[0, 0], dw2.at[0]))
+        )
+    ]
+
+    def encoded(first, blocks, plane, weight, bias):
+        value = bias[...] + jnp.zeros((blocks * 64, 1), F32)
         for h in (0, 1):
             value += jnp.dot(
-                tok[h, first : first + blocks].reshape(blocks * 128, half_width),
-                ew[h * half_width : (h + 1) * half_width],
+                tok[h, first : first + blocks, plane].reshape(blocks * 64, half_width),
+                weight[h * half_width : (h + 1) * half_width],
                 preferred_element_type=F32,
             )
-        value = jnp.maximum(value, 0.0)
-        pre[rows] = value
-        acts[rows] = (value * value).astype(BF16)
-
-    psib = {
-        (h, p): remote(
-            sib_out.at[h, pl.ds(2 * p, 2)], sib_in.at[h, pl.ds(2 * p, 2)],
-            psib_s.at[h, p], psib_r.at[h, p], sibling,
-        )
-        for h in (0, 1)
-        for p in (0, 1)
-    }
+        return jnp.maximum(value, 0.0).reshape(blocks, 64, value.shape[1])
+
+    def encode(first, blocks):
+        at = slice(first, first + blocks)
+        value = encoded(first, blocks, 0, ew, eb)
+        pre[at, 0] = value
+        acts[at, 0] = (value * value).astype(BF16)
+        value = encoded(first, blocks, 0, ew2, eb2)
+        acts2[at] = (value * value).astype(BF16)
+
+    def encode_others():
+        for h in (0, 1):
+            for b in range(4):
+                settle(h, b)
+        value = encoded(0, 4, 1, ew, eb)
+        pre[:, 1] = value
+        acts[:, 1] = (value * value).astype(BF16)
+
     tile = 512
 
-    def decode(p):
+    def decode(p, q):
         for h in (1, 0):
 
-            @pl.loop(0, width // tile)
+            @pl.loop(0, half_width // tile)
             def _(j):
                 columns = pl.ds(pl.multiple_of(j * tile, tile), tile)
+                whole = pl.ds(pl.multiple_of(q * half_width + j * tile, tile), tile)
                 value = jnp.dot(
-                    acts[pl.ds(p * 256, 256)], dw[h, :, columns], preferred_element_type=F32
-                ).reshape(2, 2, 4, 16, tile)
-                for b in (0, 1):
-                    part[h, 2 * p + b, :, :, columns] = value[b, 0]
-                    sib_out[h, 2 * p + b, :, :, columns] = value[b, 1].astype(BF16)
-
-            psib[h, p].start()
-            sent.append(psib[h, p])
+                    acts[2 * p : 2 * p + 2, 0].reshape(128, acts.shape[3]),
+                    dw[h, :, whole],
+                    preferred_element_type=F32,
+                )
+                value += jnp.dot(
+                    acts2[2 * p : 2 * p + 2].reshape(128, acts.shape[3]),
+                    dw2[h, :, whole],
+                    preferred_element_type=F32,
+                )
+                part[q, h, 2 * p : 2 * p + 2, :, :, columns] = value.reshape(2, 4, 16, tile)
 
     red = {}
-    for (h, s), (_, way) in ERROR_TREE.items():
+    for q in (0, 1):
+        for (h, s), (_, way) in ERROR_TREES[q].items():
+            b, k = PLACE[s]
+            red[q, h, s] = remote(
+                snd.at[q, h, b, k], arr.at[q, h, b, k],
+                red_s.at[q, h, b, k], red_r.at[q, h, b, k], back_to[way],
+            )
+
+    def total(q, h, s):
         b, k = PLACE[s]
-        red[h, s] = remote(
-            snd.at[h, b, k], arr.at[h, b, k], red_s.at[h, b, k], red_r.at[h, b, k], back_to[way]
-        )
-
-    def total(h, s):
-        b, k = PLACE[s]
-        value = part[h, b, k] + sib_in[h, b, k].astype(F32)
-        for child in children_of(ERROR_TREE, (h, s)):
-            red[child].wait_recv()
-            cb, ck = PLACE[child[1]]
-            term = arr[child[0], cb, ck].astype(F32)
-            if ERROR_TREE[child][1] == "cross":
+        value = part[q, h, b, k]
+        for child in children_of(ERROR_TREES[q], (h, s)):
+            ch, cs = child
+            red[q, ch, cs].wait_recv()
+            cb, ck = PLACE[cs]
+            term = arr[q, ch, cb, ck].astype(F32)
+            if ERROR_TREES[q][child][1] == "cross":
                 term = jnp.where(layer == 0, 0.0, term)
             value += term
         return value
 
-    def pass_on(h, *slots):
+    def pass_on(q, h, *slots):
         for s in slots:
             b, k = PLACE[s]
-            snd[h, b, k] = total(h, s).astype(BF16)
-            red[h, s].start()
-            sent.append(red[h, s])
+            snd[q, h, b, k] = total(q, h, s).astype(BF16)
+            red[q, h, s].start()
+            sent.append(red[q, h, s])
 
     for h in (0, 1):
         own_loads[h].wait()
         stage(h, OWN_WAVES[0])
+    for copy in copies:
+        copy.start()
+    sent += copies
     for h in (0, 1):
-        stage(h, OWN_WAVES[1])
+        stage(h, ((0, 2), (0, -2), (1, 0)))
+    for h in (0, 1):
+        stage(h, ((0, 1), (0, -1)))
     ew_load.wait()
     eb_load.wait()
     for h in (0, 1):
-        stage(h, OWN_WAVES[2])
+        stage(h, ((0, 3), (0, -3), (0, 4)))
+    for h in (0, 1):
+        stage(h, ((1, 1), (1, -1), (1, 2), (1, -2)))
+    copies[0].wait_recv()
+    copies[1].wait_recv()
     encode(0, 2)
     for load_ in dw_loads:
         load_.wait()
-    decode(0)
+    copies[2].wait_recv()
+    copies[3].wait_recv()
+    for q in (0, 1):
+        decode(0, q)
     for h in (0, 1):
         stage(h, OWN_WAVES[3])
-    psib[1, 0].wait_recv()
-    pass_on(1, (0, 2), (0, -2), (0, 1), (0, -1), (1, 1), (1, -1), (1, 0))
-    psib[0, 0].wait_recv()
-    pass_on(0, (1, 1), (1, -1))
+    for q in (0, 1):
+        pass_on(q, 1, (0, 2), (0, -2), (0, 1), (0, -1), (1, 1), (1, -1), (1, 0))
     encode(2, 2)
-    decode(1)
-    pass_on(1, (0, 0))
-    psib[1, 1].wait_recv()
-    pass_on(1, (0, 3), (0, -3), (0, 4))
-    psib[0, 1].wait_recv()
-    pass_on(0, (1, 3), (1, -3), (1, 4), (1, 2), (1, -2))
-    pass_on(1, (1, 3), (1, -3), (1, 4))
-    pass_on(0, (0, 3), (0, -3), (0, 4))
-    pass_on(0, (0, 1), (0, -1), (1, 0))
-    pass_on(1, (1, 2), (1, -2))
+    for q in (0, 1):
+        decode(1, q)
+    for q in (0, 1):
+        pass_on(q, 1, (0, 3), (0, -3), (0, 4))
+    for q in (0, 1):
+        pass_on(q, 0, (1, 3), (1, -3), (1, 4))
+    for q in (0, 1):
+        pass_on(q, 1, (0, 0))
+        pass_on(q, 0, (1, 1), (1, -1))
+    encode_others()
+    for q in (0, 1):
+        pass_on(q, 1, (1, 3), (1, -3), (1, 4))
+    for q in (0, 1):
+        pass_on(q, 0, (1, 2), (1, -2))
+    for q in (0, 1):
+        pass_on(q, 0, (0, 3), (0, -3), (0, 4))
+    for q in (0, 1):
+        pass_on(q, 1, (1, 2), (1, -2))
+    for q in (0, 1):
+        pass_on(q, 0, (0, 1), (0, -1), (1, 0))
     tg_load.wait()
     db_load.wait()
-    pass_on(0, (0, 2), (0, -2))
-    gr0[0, 0, 0] = (total(0, OWN) + db[...] - tg[...].astype(F32)).astype(BF16)
-
-    stage, settle = gather(ERROR_TREE, (gr0, gr1), gr_s, gr_r, gsib_s, gsib_r)
+    for q in (0, 1):
+        pass_on(q, 0, (0, 2), (0, -2))
+
     gr = (gr0, gr1)
+    stages, settles = [], []
+    for q in (0, 1):
+        stage, settle = gather(
+            ERROR_TREES[q], (gr0.at[q], gr1.at[q]),
+            gr_s.at[q], gr_r.at[q], gsib_s.at[q], gsib_r.at[q],
+        )
+        stages.append(stage)
+        settles.append(settle)
 
     def through(h, first, blocks):
         rows = pl.ds(first * 128, blocks * 128)
-        for b in range(first, first + blocks):
-            settle(h, b)
-        value = lax.dot_general(
-            gr[h][first : first + blocks].reshape(blocks * 128, width), dw[h],
-            (((1,), (1,)), ((), ())), preferred_element_type=F32,
-        )
+        value = back[rows] if h == 1 else 0.0
+        for q in (0, 1):
+            for b in range(first, first + blocks):
+                settles[q](h, b)
+            value += lax.dot_general(
+                gr[h][q, first : first + blocks].reshape(blocks * 128, half_width),
+                dw[h, :, q * half_width : (q + 1) * half_width],
+                (((1,), (1,)), ((), ())), preferred_element_type=F32,
+            )
         if h == 0:
             back[rows] = value
         else:
-            dpre[rows] = ((value + back[rows]) * 2.0 * pre[rows]).astype(BF16)
+            rectified = pre[first : first + blocks].reshape(value.shape)
+            dpre[rows] = (value * 2.0 * rectified).astype(BF16)
 
     def decoder_grad(p):
-        @pl.loop(0, width // tile)
-        def _(j):
-            columns = pl.ds(pl.multiple_of(j * tile, tile), tile)
-            value = lax.dot_general(
-                acts[pl.ds(p * 256, 256)],
-                gr0[2 * p : 2 * p + 2, :, :, :, columns].reshape(256, tile),
-                (((0,), (0,)), ((), ())), preferred_element_type=F32,
-            )
-            if p == 0:
-                dg_sum[:, columns] = value
-            else:
-                dg0[:, columns] = (value + dg_sum[:, columns]).astype(BF16)
+        for q in (0, 1):
+
+            @pl.loop(0, half_width // tile)
+            def _(j):
+                columns = pl.ds(pl.multiple_of(j * tile, tile), tile)
+                whole = pl.ds(pl.multiple_of(q * half_width + j * tile, tile), tile)
+                value = lax.dot_general(
+                    acts[2 * p : 2 * p + 2].reshape(256, acts.shape[3]),
+                    gr0[q, 2 * p : 2 * p + 2, :, :, :, columns].reshape(256, tile),
+                    (((0,), (0,)), ((), ())), preferred_element_type=F32,
+                )
+                if p == 0:
+                    dg_sum[:, whole] = value
+                else:
+                    dg0[:, whole] = (value + dg_sum[:, whole]).astype(BF16)
 
     def add_up():
-        @pl.loop(0, width // tile)
-        def _(j):
-            columns = pl.ds(pl.multiple_of(j * tile, tile), tile)
-            total_sum = jnp.zeros((8, tile), F32)
-            total_sq = jnp.zeros((8, tile), F32)
-            for b in range(4):
-                for p in range(2):
-                    value = gr0[b, p, :, :, columns].astype(F32).reshape(8, 8, tile)
-                    total_sum += jnp.sum(value, axis=0)
-                    total_sq += jnp.sum(value * value, axis=0)
-            sums[:, columns] = total_sum
-            squares[:, columns] = total_sq
+        for q in (0, 1):
+
+            @pl.loop(0, half_width // tile)
+            def _(j):
+                columns = pl.ds(pl.multiple_of(j * tile, tile), tile)
+                whole = pl.ds(pl.multiple_of(q * half_width + j * tile, tile), tile)
+                total_sum = jnp.zeros((8, tile), F32)
+                total_sq = jnp.zeros((8, tile), F32)
+                for b in range(4):
+                    for p in range(2):
+                        value = gr0[q, b, p, :, :, columns].astype(F32).reshape(8, 8, tile)
+                        total_sum += jnp.sum(value, axis=0)
+                        total_sq += jnp.sum(value * value, axis=0)
+                sums[:, whole] = total_sum
+                squares[:, whole] = total_sq
 
         value = jnp.zeros((8, 128), F32)
         for j in range(width // 128):
             value += squares[:, j * 128 : (j + 1) * 128]
         loss_all[0] = value
 
-    stage(0, OWN_WAVES[0])
-    stage(0, OWN_WAVES[1])
-    stage(1, NEXT_WAVES[0])
-    stage(0, OWN_WAVES[2])
-    stage(1, NEXT_WAVES[1])
+    for q in (0, 1):
+        columns = slice(q * half_width, (q + 1) * half_width)
+        error = total(q, 0, OWN) + db[:, columns] - tg[:, columns].astype(F32)
+        gr0[q, 0, 0, 0] = error.astype(BF16)
+        stages[q](0, OWN_WAVES[0])
+    for q in (0, 1):
+        stages[q](0, ((0, 2), (0, -2), (1, 0)))
+    for q in (0, 1):
+        stages[q](0, ((0, 1), (0, -1)))
+        stages[q](1, NEXT_WAVES[0])
+    for q in (0, 1):
+        stages[q](1, ((1, 2), (1, -2), (0, 0)))
+        stages[q](0, ((0, 3), (0, -3), (0, 4)))
+    for q in (0, 1):
+        stages[q](0, ((1, 1), (1, -1), (1, 2), (1, -2)))
+        stages[q](1, ((1, 1), (1, -1)))
     through(0, 0, 2)
     decoder_grad(0)
-    stage(0, OWN_WAVES[3])
-    stage(1, NEXT_WAVES[2])
+    for q in (0, 1):
+        stages[q](1, ((1, 3), (1, -3), (1, 4)))
+    for q in (0, 1):
+        stages[q](0, OWN_WAVES[3])
+        stages[q](1, ((0, 1), (0, -1), (0, 2), (0, -2)))
     through(0, 2, 2)
     add_up()
     tells = []
@@ -341,7 +412,8 @@
         )
         tells[-1].start()
     decoder_grad(1)
-    stage(1, NEXT_WAVES[3])
+    for q in (0, 1):
+        stages[q](1, NEXT_WAVES[3])
     through(1, 0, 3)
     through(1, 3, 1)
     for tell in tells:
@@ -378,11 +450,10 @@
     dbg[...] = jnp.sum(sums[...], axis=0, keepdims=True)
     store(ebg, ebg_o)
     store(dbg, dbg_o)
-    for j in range(gr1.shape[1] // tile):
+    for j in range(2 * half_width // tile):
         at = j * tile
-        dg[j] = lax.dot_general(
-            acts[...], gr1[:, at : at + tile], contract, preferred_element_type=F32
-        ).astype(BF16)
+        part = gr1[at // half_width, :, at % half_width : at % half_width + tile]
+        dg[j] = lax.dot_general(acts[...], part, contract, preferred_element_type=F32).astype(BF16)
         store(dg.at[j], dg_o.at[0, 1, :, pl.ds(at, tile)])
     mean[0, 0] = jnp.sum(loss[...]) * scale
     for copy in copies:
@@ -402,8 +473,8 @@
         main_kernel,
         out_shape=(
             pltpu.VMEM((2, *chunks, half_width), BF16),
-            pltpu.VMEM((tokens, feats), BF16),
-            pltpu.VMEM((*chunks, width), BF16),
+            pltpu.VMEM((4, 2, tokens // 8, feats), BF16),
+            pltpu.VMEM((2, *chunks, half_width), BF16),
             pltpu.VMEM((tokens, feats), BF16),
             pltpu.VMEM((feats, width), BF16),
             pltpu.VMEM((8, width), F32),
@@ -415,25 +486,26 @@
             pltpu.VMEM((width, feats), BF16),
             pltpu.VMEM((2, feats, width), BF16),
             pltpu.VMEM((1, feats), F32),
+            pltpu.VMEM((width, feats), BF16),
+            pltpu.VMEM((2, feats, width), BF16),
+            pltpu.VMEM((1, feats), F32),
             pltpu.VMEM((1, width), F32),
             pltpu.VMEM((rows, width), BF16),
-            pltpu.VMEM((tokens, feats), F32),
-            pltpu.VMEM((2, 4, 4, rows, width), F32),
-            pltpu.VMEM((2, 4, 4, rows, width), BF16),
-            pltpu.VMEM((2, 4, 4, rows, width), BF16),
-            pltpu.VMEM((2, 4, 4, rows, width), BF16),
-            pltpu.VMEM((2, 4, 4, rows, width), BF16),
-            pltpu.VMEM((rows, width), BF16),
-            pltpu.VMEM((*chunks, width), BF16),
+            pltpu.VMEM((4, 2, tokens // 8, feats), F32),
+            pltpu.VMEM((4, tokens // 8, feats), BF16),
+            pltpu.VMEM((2, 2, 4, 4, rows, half_width), F32),
+            pltpu.VMEM((2, 2, 4, 4, rows, half_width), BF16),
+            pltpu.VMEM((2, 2, 4, 4, rows, half_width), BF16),
+            pltpu.VMEM((rows, half_width), BF16),
+            pltpu.VMEM((2, *chunks, half_width), BF16),
             pltpu.VMEM((tokens, feats), F32),
             pltpu.VMEM((feats, width), F32),
             pltpu.VMEM((8, width), F32),
             pltpu.VMEM((2 * NX, 8, 128), F32),
             dma((8,)),
             *[dma((2, 4, 4))] * 4,
-            *[dma((2, 2))] * 2,
-            *[dma((2, 4, 4))] * 2,
-            *[dma((2, 4, 4))] * 4,
+            *[dma((4,))] * 2,
+            *[dma((2, 2, 4, 4))] * 6,
             *[dma((2 * NX - 1,))] * 2,
         ],
         compiler_params=pltpu.CompilerParams(
@@ -442,7 +514,8 @@
         name="exchange",
     )(inputs, targets, enc_weight, enc_bias, dec_weight, dec_bias)
     tok = tok.reshape(2, tokens, half_width)
-    gr1 = gr1.reshape(tokens, width)
+    acts = acts.reshape(tokens, feats)
+    gr1 = gr1.reshape(2, tokens, half_width)
     scale = 1.0 / (2 * NX * tokens * width)
     eg, ebg, dg, dbg, mean = pl.pallas_call(
         lambda *refs: grad_kernel(scale, *refs),

time: 83.9 us -> 79.9 us (0.952)
  Pallas kernels: 83.2 us -> 79 us
    pallas_call x1, Pallas kernels: 79.4 us -> 75.2 us  [shards(): pl.pallas_call(main_kernel, out_shape=(pltpu.VMEM((2, *chunks, half_width...]
where the time goes in v4:
time: 79.9 us; the launch traced here: 79.6 us
  Pallas kernels  79 us (99%)
    pallas_call x1, Pallas kernels, shards(): pl.pallas_call(main_kernel, out_shape=(pltpu.VMEM((2, *chunks, half_width...  75.2 us
    pallas_call x1, Pallas kernels, shards(): pl.pallas_call(lambda *refs: grad_kernel(scale, *refs), out_shape=(jax.Sh...  3.8 us

profile of v4, /device:TPU:1, one launch (start us, length us, event | category | flops | bytes accessed | tf_op | source)
XLA Modules:
  0.0 79.6 jit_solution(7476094756803703062)
XLA Ops:
  0.6 75.2 %exchange.1 = (bf16[2,4,2,4,16,1024]{5,4,3,2,1,0:T(8,128)(2,1)S(1)}, bf16[4,2,64,512]{3,2,1,0:T(8,128)(2,1)S(1)}, bf16[2,4,2,4,16,1024]{5,4,3,2,1,0:T(8,128)(2,1...) custom-call(bf16[1,16,2048]{2,1,0:T(8,128)(2,1)} %x_hbm.1, ...), custom_call_target="tpu_custom_call" | custom-call | tf_op jit(solution)/shard_map/exchange/pallas_call | solution.py:472
  75.8 3.8 %weight_grads.1 = (bf16[1,2048,512]{2,1,0:T(8,128)(2,1)}, f32[1,512]{1,0:T(1,128)}, bf16[1,2,512,2048]{3,2,1,0:T(8,128)(2,1)}, f32[1,2048]{1,0:T(1,128)}, f32[1,1]{1,0:T(1,128)}) custom-call(bf16[2,512,1024]{2,1,0:T(8,128)(2,1)S(1)} %bitcast.4, bf16[512,512]{1,0:T(8,128)(2,1)S(1)} %bitcast.6, bf16[2,512,1024]{2,1,0:T(8,128)(2,1)S(1)} %bitcast.5, ...), custom_call_target="tpu_custom_call" | custom-call | tf_op jit(solution)/shard_map/weight_grads/pallas_call | solution.py:520

commit v5 on v4

--- a/solution.py
+++ b/solution.py
@@ -211,8 +211,8 @@
 
     tile = 512
 
-    def decode(p, q):
-        for h in (1, 0):
+    def decode(p, q, halves=(1, 0)):
+        for h in halves:
 
             @pl.loop(0, half_width // tile)
             def _(j):
@@ -283,30 +283,32 @@
     copies[2].wait_recv()
     copies[3].wait_recv()
     for q in (0, 1):
-        decode(0, q)
+        decode(0, q, (1,))
+        pass_on(q, 1, (0, 2), (0, -2), (0, 1), (0, -1), (1, 1), (1, -1), (1, 0))
     for h in (0, 1):
         stage(h, OWN_WAVES[3])
-    for q in (0, 1):
-        pass_on(q, 1, (0, 2), (0, -2), (0, 1), (0, -1), (1, 1), (1, -1), (1, 0))
     encode(2, 2)
     for q in (0, 1):
-        decode(1, q)
-    for q in (0, 1):
+        decode(1, q, (1,))
         pass_on(q, 1, (0, 3), (0, -3), (0, 4))
     for q in (0, 1):
+        decode(1, q, (0,))
+    for q in (0, 1):
         pass_on(q, 0, (1, 3), (1, -3), (1, 4))
+    for q in (0, 1):
+        decode(0, q, (0,))
     for q in (0, 1):
         pass_on(q, 1, (0, 0))
         pass_on(q, 0, (1, 1), (1, -1))
+    for q in (0, 1):
+        pass_on(q, 1, (1, 3), (1, -3), (1, 4))
+    for q in (0, 1):
+        pass_on(q, 0, (1, 2), (1, -2))
+    for q in (0, 1):
+        pass_on(q, 0, (0, 3), (0, -3), (0, 4))
+    for q in (0, 1):
+        pass_on(q, 1, (1, 2), (1, -2))
     encode_others()
-    for q in (0, 1):
-        pass_on(q, 1, (1, 3), (1, -3), (1, 4))
-    for q in (0, 1):
-        pass_on(q, 0, (1, 2), (1, -2))
-    for q in (0, 1):
-        pass_on(q, 0, (0, 3), (0, -3), (0, 4))
-    for q in (0, 1):
-        pass_on(q, 1, (1, 2), (1, -2))
     for q in (0, 1):
         pass_on(q, 0, (0, 1), (0, -1), (1, 0))
     tg_load.wait()

time: 79.9 us -> 77.2 us (0.966)
  Pallas kernels: 79 us -> 76.3 us
    pallas_call x1, Pallas kernels: 75.2 us -> 72.5 us  [shards(): pl.pallas_call(main_kernel, out_shape=(pltpu.VMEM((2, *chunks, half_width...]
where the time goes in v5:
time: 77.2 us; the launch traced here: 76.9 us
  Pallas kernels  76.3 us (99%)
    pallas_call x1, Pallas kernels, shards(): pl.pallas_call(main_kernel, out_shape=(pltpu.VMEM((2, *chunks, half_width...  72.5 us
    pallas_call x1, Pallas kernels, shards(): pl.pallas_call(lambda *refs: grad_kernel(scale, *refs), out_shape=(jax.Sh...  3.8 us

profile of v5, /device:TPU:1, one launch (start us, length us, event | category | flops | bytes accessed | tf_op | source)
XLA Modules:
  0.0 76.9 jit_solution(5939690154034988191)
XLA Ops:
  0.6 72.5 %exchange.1 = (bf16[2,4,2,4,16,1024]{5,4,3,2,1,0:T(8,128)(2,1)S(1)}, bf16[4,2,64,512]{3,2,1,0:T(8,128)(2,1)S(1)}, bf16[2,4,2,4,16,1024]{5,4,3,2,1,0:T(8,128)(2,1...) custom-call(bf16[1,16,2048]{2,1,0:T(8,128)(2,1)} %x_hbm.1, ...), custom_call_target="tpu_custom_call" | custom-call | tf_op jit(solution)/shard_map/exchange/pallas_call | solution.py:474
  73.1 3.8 %weight_grads.1 = (bf16[1,2048,512]{2,1,0:T(8,128)(2,1)}, f32[1,512]{1,0:T(1,128)}, bf16[1,2,512,2048]{3,2,1,0:T(8,128)(2,1)}, f32[1,2048]{1,0:T(1,128)}, f32[1,1]{1,0:T(1,128)}) custom-call(bf16[2,512,1024]{2,1,0:T(8,128)(2,1)S(1)} %bitcast.4, bf16[512,512]{1,0:T(8,128)(2,1)S(1)} %bitcast.6, bf16[2,512,1024]{2,1,0:T(8,128)(2,1)S(1)} %bitcast.5, ...), custom_call_target="tpu_custom_call" | custom-call | tf_op jit(solution)/shard_map/weight_grads/pallas_call | solution.py:522
